TPU v7x, 32 devices: a whole 2x2x4 slice. The times are simulated.
32 devices in a mesh: seg: 8 (over z, x), mp: 4 (over y, core).
Axes of the slice: x: 2, y: 2, z: 4, core: 2. Of those that a mesh axis runs over, the one named last changes fastest.
Arguments:
- patches: bfloat16 [8192, 768], P('seg'), may hold values from -6 to 6
- curve_owner: int32 [8192], P('seg'), may hold values from 0 to 7, as said below
- arrival_slot: int32 [8192], P('seg'), may hold values from 0 to 2047, as said below
- patch_level: int32 [8192], P('seg'), may hold values from 0 to 3
- neighbours: int32 [8192, 16], P('seg'), may hold values from 0 to 8191, as said below
- level_embed: bfloat16 [4, 768], replicated, may hold values from -3 to 3
- norm_gain: float32 [768], replicated, may hold values from 0.5 to 2
- qkv_weight: bfloat16 [768, 3, 768], P(None, None, 'mp')
- out_weight: bfloat16 [768, 768], P('mp'), may hold values from -0.21875 to 0.21875
- cotangent: bfloat16 [8192, 768], P('seg'), may hold values from -6 to 6
Outputs:
- token_grads: float32 [8192, 768], P('seg', 'mp')
- qkv_grad: float32 [768, 3, 768], P(None, None, 'mp')
- out_grad: float32 [768, 768], P('mp')
- gain_grad: float32 [768], P('mp')
Inputs may be any that keep to these rules, and one draw needn't show every extreme that they name: `curve_owner`: every device owns exactly 1024 patches. No device holds more than 256 patches with one owner, and in every draw some device holds exactly 256 patches with some owner. `arrival_slot`: entry d * 1024 + p is s * 256 + k: the patch at position p of owner d is the k-th, counted from 0 in row order, of the rows of device s whose owner is d. The entries of one owner are distinct and name every patch it owns. `neighbours`: row p lists positions within 128 of p on the curve, p itself among them; a position may repeat.
All inputs are finite; a program needn't handle non-finite values.
Results may differ from a plain program's by a relative error of at most 0.029.
Values may be sent and summed in bfloat16 or wider, within the bound.
A program may use at most 64 MiB of HBM per device.

v0:
```python
import jax
import jax.numpy as jnp
from jax import lax
from jax.sharding import PartitionSpec as P

DH = 64
R = 128


EPSILON = 1e-06


def with_halo(cells, sides, width):
    for axis, dim in sides:
        count = lax.axis_size(axis)
        ends = count - 1
        head = lax.slice_in_dim(cells, 0, width, axis=dim)
        tail = lax.slice_in_dim(cells, cells.shape[dim] - width, cells.shape[dim], axis=dim)
        cells = jnp.concatenate(
            [
                lax.ppermute(tail, axis, [(i, (i + 1) % count) for i in range(ends)]),
                cells,
                lax.ppermute(head, axis, [((i + 1) % count, i) for i in range(ends)]),
            ],
            axis=dim,
        )
    return cells


def per_device(
    patches,
    curve_owner,
    arrival_slot,
    patch_level,
    neighbours,
    level_embed,
    norm_gain,
    qkv_weight,
    out_weight,
    cotangent,
):
    segments = lax.axis_size("seg")
    shares = lax.axis_size("mp")
    tok_rows = patches.shape[0]
    model_width = patches.shape[1]
    local_width = qkv_weight.shape[2]
    heads_here = local_width // DH
    capacity = 2 * tok_rows // segments
    share_width = model_width // shares
    first_column = lax.axis_index("mp") * share_width
    onehot = (curve_owner[:, None] == jnp.arange(segments, dtype=jnp.int32)[None, :]).astype(
        jnp.int32
    )
    row_ranks = jnp.sum(onehot * (jnp.cumsum(onehot, axis=0) - onehot), axis=1)
    slot_index = curve_owner * capacity + row_ranks
    columns_here = patches.shape[1]
    buffer = (
        jnp.zeros((segments * capacity, columns_here), patches.dtype).at[slot_index].set(patches)
    )
    arrived = lax.all_to_all(
        buffer.reshape(segments, capacity, columns_here),
        "seg",
        split_axis=0,
        concat_axis=0,
        tiled=True,
    )
    routed = arrived.reshape(segments * capacity, columns_here)[arrival_slot]
    levels_count = level_embed.shape[0]
    level_hot = (patch_level[:, None] == jnp.arange(levels_count, dtype=jnp.int32)[None, :]).astype(
        jnp.bfloat16
    )
    embedded = routed.astype(jnp.float32) + jnp.dot(
        level_hot, level_embed, preferred_element_type=jnp.float32
    )
    inv_rms = lax.rsqrt(jnp.mean(embedded * embedded, axis=1, keepdims=True) + EPSILON)
    normed = embedded * inv_rms
    hidden = (normed * norm_gain).astype(jnp.bfloat16)
    flat_weight = qkv_weight.reshape(model_width, 3 * local_width)
    project = jnp.dot(hidden, flat_weight, preferred_element_type=jnp.float32).astype(jnp.bfloat16)
    queries = project[:, :local_width]
    key_value = project[:, local_width:]
    extended = with_halo(key_value, (("seg", 0),), R)
    grad_out = lax.dot_general(
        cotangent, out_weight, (((1,), (1,)), ((), ())), preferred_element_type=jnp.float32
    ).astype(jnp.bfloat16)
    block_rows = min(tok_rows, 512)
    key_span = block_rows + 2 * R
    score_scale = DH ** (-0.5)
    first_key = lax.axis_index("seg") * tok_rows - R
    grad_ext = jnp.zeros((tok_rows + 2 * R, 2 * local_width), jnp.float32)
    outputs = []
    query_grads = []
    for block_index in range(tok_rows // block_rows):
        block_start = block_index * block_rows
        query_block = queries[block_start : block_start + block_rows].reshape(
            block_rows, heads_here, DH
        )
        pair_block = extended[block_start : block_start + key_span].reshape(
            key_span, 2, heads_here, DH
        )
        key_block = pair_block[:, 0]
        value_block = pair_block[:, 1]
        positions = first_key + block_start + jnp.arange(key_span, dtype=jnp.int32)
        listed = neighbours[block_start : block_start + block_rows]
        allowed = listed[:, 0:1] == positions[None, :]
        for column in range(1, listed.shape[1]):
            allowed = allowed | (listed[:, column : column + 1] == positions[None, :])
        allowed = allowed[None]
        scores = (
            jnp.einsum("qhd,khd->hqk", query_block, key_block, preferred_element_type=jnp.float32)
            * score_scale
        )
        row_top = jnp.max(jnp.where(allowed, scores, -jnp.inf), axis=2, keepdims=True)
        exponent = jnp.where(allowed, jnp.exp(scores - row_top), 0.0)
        probability = exponent / jnp.sum(exponent, axis=2, keepdims=True)
        weights = probability.astype(jnp.bfloat16)
        out_block = jnp.einsum(
            "hqk,khd->qhd", weights, value_block, preferred_element_type=jnp.float32
        ).astype(jnp.bfloat16)
        grad_block = grad_out[block_start : block_start + block_rows].reshape(
            block_rows, heads_here, DH
        )
        row_delta = jnp.sum(
            grad_block.astype(jnp.float32) * out_block.astype(jnp.float32), axis=2
        ).T[:, :, None]
        grad_prob = jnp.einsum(
            "qhd,khd->hqk", grad_block, value_block, preferred_element_type=jnp.float32
        )
        dscore = (probability * (grad_prob - row_delta) * score_scale).astype(jnp.bfloat16)
        dquery = jnp.einsum("hqk,khd->qhd", dscore, key_block, preferred_element_type=jnp.float32)
        grad_key = jnp.einsum(
            "hqk,qhd->khd", dscore, query_block, preferred_element_type=jnp.float32
        )
        dvalue = jnp.einsum("hqk,qhd->khd", weights, grad_block, preferred_element_type=jnp.float32)
        joined = jnp.concatenate(
            [grad_key.reshape(key_span, local_width), dvalue.reshape(key_span, local_width)], axis=1
        )
        grad_ext = grad_ext.at[block_start : block_start + key_span].add(joined)
        outputs.append(out_block.reshape(block_rows, local_width))
        query_grads.append(dquery.reshape(block_rows, local_width))
    rim_rows = jnp.concatenate([grad_ext[:R], grad_ext[tok_rows + R :]], axis=0)
    returned = with_halo(rim_rows, (("seg", 0),), R)
    grad_kv = (
        grad_ext[R : R + tok_rows]
        .at[:R]
        .add(returned[:R])
        .at[tok_rows - R :]
        .add(returned[3 * R :])
    )
    grad_qkv = jnp.concatenate([jnp.concatenate(query_grads, axis=0), grad_kv], axis=1).astype(
        jnp.bfloat16
    )
    attended = jnp.concatenate(outputs, axis=0)
    qkv_part = lax.dot_general(
        hidden, grad_qkv, (((0,), (0,)), ((), ())), preferred_element_type=jnp.float32
    )
    out_part = lax.dot_general(
        attended, cotangent, (((0,), (0,)), ((), ())), preferred_element_type=jnp.float32
    )
    hidden_part = lax.dot_general(
        grad_qkv, flat_weight, (((1,), (1,)), ((), ())), preferred_element_type=jnp.float32
    )
    grad_hidden = lax.psum(hidden_part, "mp")
    scaled = grad_hidden * norm_gain
    full_grads = cotangent.astype(jnp.float32) + inv_rms * (
        scaled - normed * jnp.mean(scaled * normed, axis=1, keepdims=True)
    )
    token_grads = lax.dynamic_slice_in_dim(full_grads, first_column, share_width, 1)
    gain_part = lax.dynamic_slice_in_dim(
        jnp.sum(grad_hidden * normed, axis=0), first_column, share_width, 0
    )
    summed_qkv, summed_out, summed_gain = lax.psum((qkv_part, out_part, gain_part), "seg")
    factor = (tok_rows * segments) ** (-0.5)
    qkv_grad = (summed_qkv * factor).reshape(model_width, 3, local_width)
    return (token_grads, qkv_grad, summed_out * factor, summed_gain * factor)


def solution(mesh):
    placed = (
        P("seg", None),
        P("seg"),
        P("seg"),
        P("seg"),
        P("seg", None),
        P(),
        P(),
        P(None, None, "mp"),
        P("mp", None),
        P("seg", None),
    )
    return jax.shard_map(
        per_device,
        mesh=mesh,
        in_specs=placed,
        out_specs=(P("seg", "mp"), P(None, None, "mp"), P("mp", None), P("mp")),
        check_vma=False,
    )
```

profile of v0, /device:TPU:0, one launch (start us, length us, event | category | flops | bytes accessed | tf_op | source)
XLA Modules:
  0.0 360.0 jit_solution(1146869149718708248)
XLA Ops:
  7.2 0.8 fusion.42
  8.0 2.3 reduce-window.6
  10.8 0.7 fusion.41
  11.5 0.7 compare_select_fusion.1
  12.2 7.9 %scatter_custom_fusion = bf16[2048,768]{1,0:T(8,128)(2,1)} fusion(s32[1024]{0:T(1024)S(1)} %compare_select_fusion.1, bf16[1024,768]{1,0:T(8,128)(2,1)} %param.18, bf16[]{:T(256)} %constant.136.clone.1), kind=kCustom, calls=%fused_computation.33 | custom fusion | bytes 3146240 | tf_op jit(solution)/shard_map/scatter | solution.py:58
  20.1 7.4 %all-to-all-start = ((bf16[8,256,768]{2,1,0:T(8,128)(2,1)}), bf16[8,256,768]{2,1,0:T(8,128)(2,1)}, u32[]{:S(2)}, u32[]{:S(2)}) async-start(bf16[8,256,768]{2,1,0:T(8,128)(2,1)} %bitcast.153), calls=%async_computation | async-start | bytes 6291456 | tf_op jit(solution)/shard_map/all_to_all | solution.py:60
  27.7 0.7 convolution_convert_fusion.1
  28.4 0.7 fusion.54
  29.1 4.8 %compare_or_fusion = pred[512,768]{1,0:T(8,128)(4,1)} fusion(s32[768]{0:T(1024)S(1)} %iota_add_fusion, s32[512]{0:T(512)S(1)} %bitcast.222, s32[512]{0:T(512)S(1)} %bitcast.221, s32[512]{0:T(512)S(1)} %bitcast.197, s32[512]{0:T(512)S(1)} %bitcast.198, s32[512]{0:T(512)S(1)} %bitcast.199, s32[512]{0:T(512)S(1)} %bitcast.200, s32[512]{0:T(512)S(1)} %bitcast.201, ...), kind=kLoop, calls=%fused_computation.35 | loop fusion | flops 12189696 | bytes 429056 | tf_op jit(solution)/shard_map/or | solution.py:107
  33.9 4.8 %compare_or_fusion.1 = pred[512,768]{1,0:T(8,128)(4,1)} fusion(s32[768]{0:T(1024)S(1)} %iota_add_fusion.1, s32[512]{0:T(512)S(1)} %bitcast.191, s32[512]{0:T(512)S(1)} %bitcast.192, s32[512]{0:T(512)S(1)} %bitcast.193, s32[512]{0:T(512)S(1)} %bitcast.194, s32[512]{0:T(512)S(1)} %bitcast.195, s32[512]{0:T(512)S(1)} %bitcast.210, s32[512]{0:T(512)S(1)} %bitcast.211, ...), kind=kLoop, calls=%fused_computation.36 | loop fusion | flops 12189696 | bytes 429056 | tf_op jit(solution)/shard_map/or | solution.py:107
  38.6 59.7 %all-to-all-done = bf16[8,256,768]{2,1,0:T(8,128)(2,1)} async-done(((bf16[8,256,768]{2,1,0:T(8,128)(2,1)}), bf16[8,256,768]{2,1,0:T(8,128)(2,1)}, u32[]{:S(2)}, u32[]{:S(2)}) %all-to-all-start) | async-done | bytes 3145760 | tf_op jit(solution)/shard_map/all_to_all | solution.py:60
  98.3 7.9 %gather_fusion = bf16[1024,768]{1,0:T(8,128)(2,1)} fusion(bf16[2048,768]{1,0:T(8,128)(2,1)} %bitcast.3, s32[1024]{0:T(1024)S(1)} %fusion.43), kind=kCustom, calls=%fused_computation | custom fusion | bytes 3149824 | tf_op jit(solution)/shard_map/gather | solution.py:67
  106.2 1.7 copy.18
  107.9 1.3 multiply_reduce_fusion.2
  109.3 0.8 fusion.16
  110.5 1.2 convolution_convert_fusion
  111.7 1.3 collective-permute-start.1
  113.0 4.7 %collective-permute-start = (bf16[128,384]{0,1:T(8,128)(2,1)S(1)}, bf16[128,384]{0,1:T(8,128)(2,1)S(1)}, u32[]{:S(2)}, u32[]{:S(2)}) collective-permute-start(bf16[128,384]{0,1:T(8,128)(2,1)S(1)} %get-tuple-element.62), channel_id=1, source_target_pairs={{0,4},{4,8},{8,12},{12,16},{16,20},{20,24},{24,28},{1,5},{5,9},{9,... | collective-permute-start | bytes 294920 | tf_op jit(solution)/shard_map/ppermute | solution.py:21
  117.8 0.7 fusion.53
  118.6 1.2 collective-permute-done
  119.9 5.7 %fusion.57 = (f32[3,512]{1,0:T(4,128)S(1)}, f32[3,512,768]{2,1,0:T(8,128)}) fusion(pred[512,768]{1,0:T(8,128)(4,1)} %compare_or_fusion.1, bf16[512,3,64]{0,2,1:T(8,128)(2,1)S(1)} %bitcast.181, bf16[768,2,3,64]{0,3,2,1:T(8,128)(2,1)S(1)} %bitcast.164), kind=kOutput, calls=%fused_computation.108 | convolution fusion | flops 309068544 | bytes 6494208 | tf_op jit(solution)/shard_map/sub | solution.py:114
  125.6 2.7 fusion.17
  128.3 1.5 multiply_reduce_fusion.4
  129.8 1.3 fusion.60
  131.2 5.7 %fusion.58 = (f32[3,512]{1,0:T(4,128)S(1)}, f32[3,512,768]{2,1,0:T(8,128)}) fusion(pred[512,768]{1,0:T(8,128)(4,1)} %compare_or_fusion, bf16[512,3,64]{0,2,1:T(8,128)(2,1)} %bitcast.179, bf16[768,2,3,64]{0,3,2,1:T(8,128)(2,1)S(1)} %bitcast.160), kind=kOutput, calls=%fused_computation.109 | convolution fusion | flops 309068544 | bytes 6494208 | tf_op jit(solution)/shard_map/sub | solution.py:114
  136.9 2.8 fusion.18
  139.8 1.5 multiply_reduce_fusion.3
  141.9 1.2 multiply_convert_fusion.1
  143.1 0.5 fusion.59
  144.2 1.4 multiply_convert_fusion
  147.2 4.3 %collective-permute-start.2 = (f32[128,384]{0,1:T(8,128)S(1)}, f32[128,384]{0,1:T(8,128)S(1)}, u32[]{:S(2)}, u32[]{:S(2)}) collective-permute-start(f32[128,384]{0,1:T(8,128)S(1)} %slice.336), channel_id=1, source_target_pairs={{0,4},{4,8},{8,12},{12,16},{16,20},{20,24},{24,28},{1,5},{5,9},{9,... | collective-permute-start | bytes 589832 | tf_op jit(solution)/shard_map/ppermute | solution.py:21
  151.7 0.8 convolution_convert_fusion.4
  152.6 2.1 collective-permute-done.2
  154.7 1.4 collective-permute-start.3
  156.2 0.8 convolution_convert_fusion.2
  157.0 6.7 %collective-permute-done.3 = f32[128,384]{0,1:T(8,128)S(1)} collective-permute-done((f32[128,384]{0,1:T(8,128)S(1)}, f32[128,384]{0,1:T(8,128)S(1)}, u32[]{:S(2)}, u32[]{:S(2)}) %collective-permute-start.3) | collective-permute-done | bytes 196640 | tf_op jit(solution)/shard_map/ppermute | solution.py:23
  163.8 3.1 fusion.29
  167.3 0.6 copy-done.5
  168.0 1.3 fusion.30
  169.3 4.3 %fusion.28 = f32[768,576]{0,1:T(8,128)} fusion(bf16[1024,384]{0,1:T(8,128)(2,1)S(1)} %convert.16, bf16[512,192]{0,1:T(8,128)(2,1)S(1)} %bitcast.186, bf16[512,192]{0,1:T(8,128)(2,1)S(1)} %bitcast.184, f32[1024,768]{0,1:T(8,128)} %copy-done.1, f32[768]{0:T(1024)S(1)} %copy-done.13), kind=kOutput, calls=%fused_computation.56 | convolution fusion | flops 911081472 | bytes 6097920 | tf_op jit(solution)/shard_map/dot_general | solution.py:154
  174.0 62.2 %all-reduce.5.cloned.1.call-done = f32[1024,768]{0,1:T(8,128)} async-done(((f32[1024,768]{0,1:T(8,128)}), f32[1024,768]{0,1:T(8,128)}) %all-reduce.5.cloned.1.call-update) | async-done | bytes 3145744 | tf_op jit(solution)/shard_map/psum | solution.py:163
  236.2 5.2 %multiply_reduce_fusion = (f32[768]{0:T(1024)S(1)}, f32[1024]{0:T(1024)S(1)}, f32[1024,768]{0,1:T(8,128)}) fusion(f32[1024,768]{0,1:T(8,128)} %all-reduce.5.cloned.1.call-done, f32[1024,768]{0,1:T(8,128)} %copy-done.1, f32[768]{0:T(1024)S(1)} %copy-done.13), kind=kLoop, calls=%fused_computation.14 | loop fusion | flops 3930368 | bytes 9447424 | tf_op jit(solution)/shard_map/reduce_sum | solution.py:170
  241.5 22.3 %psum.31 = f32[192]{0:T(256)S(1)} all-reduce(f32[192]{0:T(256)S(1)} %dynamic_slice.7), channel_id=1, replica_groups=mesh['seg'=8,'mp'=4] {'seg'}, use_global_device_ids=true, to_apply=%region_16.17 | all-reduce | flops 192 | bytes 1536 | tf_op jit(solution)/shard_map/psum | solution.py:172
  263.8 0.6 broadcast_multiply_fusion.4
  264.4 2.5 fusion.22
  266.9 82.6 %all-reduce.7.cloned.1.call-done = (f32[768,576]{0,1:T(8,128)}, f32[192,768]{1,0:T(8,128)}) async-done(((f32[768,576]{0,1:T(8,128)}, f32[192,768]{1,0:T(8,128)}), (f32[768,576]{0,1:T(8,128)}, f32[192,768]{1,0:T(8,128)})) %all-reduce.7.cloned.1.call-update) | async-done | bytes 2359312 | tf_op jit(solution)/shard_map/psum | solution.py:172
  349.4 2.9 broadcast_multiply_fusion.1
  352.3 0.9 broadcast_multiply_fusion.2
  (77 shorter events, 5.3 us)
Async XLA Ops:
  7.2 20.5 %copy-start = (bf16[1024,768]{1,0:T(8,128)(2,1)S(1)}, bf16[1024,768]{1,0:T(8,128)(2,1)}, u32[]{:S(2)}) copy-start(bf16[1024,768]{1,0:T(8,128)(2,1)} %param.27) | copy-start | bytes 4718596
  20.1 7.5 %copy-start.15 = (s32[1024]{0:T(1024)S(1)}, s32[1024]{0:T(1024)}, u32[]{:S(2)}) copy-start(s32[1024]{0:T(1024)} %param.20) | copy-start | bytes 12292
  20.1 7.5 %copy-start.11 = (s32[1024,16]{0,1:T(8,128)S(1)}, s32[1024,16]{0,1:T(8,128)}, u32[]{:S(2)}) copy-start(s32[1024,16]{0,1:T(8,128)} %param.22) | copy-start | bytes 196612
  20.1 7.6 %copy-start.18 = (bf16[192,768]{1,0:T(8,128)(2,1)S(1)}, bf16[192,768]{1,0:T(8,128)(2,1)}, u32[]{:S(2)}) copy-start(bf16[192,768]{1,0:T(8,128)(2,1)} %param.26) | copy-start | bytes 884740
  20.1 78.2 %all-to-all-start = ((bf16[8,256,768]{2,1,0:T(8,128)(2,1)}), bf16[8,256,768]{2,1,0:T(8,128)(2,1)}, u32[]{:S(2)}, u32[]{:S(2)}) async-start(bf16[8,256,768]{2,1,0:T(8,128)(2,1)} %bitcast.153), calls=%async_computation | async-start | bytes 6291456 | tf_op jit(solution)/shard_map/all_to_all | solution.py:60
  27.5 208.7 %all-reduce.5.cloned.1.call-start = ((), (), s32[]{:S(2)}) async-start(), calls=%async_computation.1 | async-start | bytes 6291456 | tf_op jit(solution)/shard_map/psum | solution.py:163
  106.2 1.8 copy-start.12
  106.2 1.8 copy-start.14
  109.3 0.8 copy-start.13
  109.3 1.2 copy-start.16
  110.1 1.6 copy-start.1
  111.7 6.8 %collective-permute-start.1 = (bf16[128,384]{0,1:T(8,128)(2,1)S(1)}, bf16[128,384]{0,1:T(8,128)(2,1)S(1)}, u32[]{:S(2)}, u32[]{:S(2)}) collective-permute-start(bf16[128,384]{0,1:T(8,128)(2,1)S(1)} %get-tuple-element.61), channel_id=1, source_target_pairs={{4,0},{8,4},{12,8},{16,12},{20,16},{24,20},{28,24},{5,1},{9,5},{13... | collective-permute-start | bytes 294920 | tf_op jit(solution)/shard_map/ppermute | solution.py:23
  113.0 6.8 %collective-permute-start = (bf16[128,384]{0,1:T(8,128)(2,1)S(1)}, bf16[128,384]{0,1:T(8,128)(2,1)S(1)}, u32[]{:S(2)}, u32[]{:S(2)}) collective-permute-start(bf16[128,384]{0,1:T(8,128)(2,1)S(1)} %get-tuple-element.62), channel_id=1, source_target_pairs={{0,4},{4,8},{8,12},{12,16},{16,20},{20,24},{24,28},{1,5},{5,9},{9,... | collective-permute-start | bytes 294920 | tf_op jit(solution)/shard_map/ppermute | solution.py:21
  118.5 7.1 %copy-start.8 = (bf16[512,192]{0,1:T(8,128)(2,1)}, bf16[512,192]{0,1:T(8,128)(2,1)S(1)}, u32[]{:S(2)}) copy-start(bf16[512,192]{0,1:T(8,128)(2,1)S(1)} %get-tuple-element.64) | copy-start | bytes 589828
  125.6 2.7 copy-start.3
  131.2 10.6 %slice-start = ((s8[4718592]{0:T(1024)(128)(4,1)}), s8[524288]{0:T(1024)(128)(4,1)S(1)}, s32[]{:S(2)}) async-start(s8[4718592]{0:T(1024)(128)(4,1)} %bitcast.154), calls=%async_computation.3 | async-start | bytes 1048576
  136.9 4.9 %slice-start.1 = ((s8[4718592]{0:T(1024)(128)(4,1)}), s8[4194304]{0:T(1024)(128)(4,1)S(1)}, s32[]{:S(2)}) async-start(s8[4718592]{0:T(1024)(128)(4,1)} %bitcast.154), calls=%async_computation.4 | async-start | bytes 8388608
  139.8 2.1 copy-start.4
  141.3 2.4 slice-start.2
  141.8 1.3 copy-start.9
  141.9 2.3 slice-start.3
  144.2 1.4 copy-start.7
  145.5 1.1 copy-start.2
  147.2 7.5 %collective-permute-start.2 = (f32[128,384]{0,1:T(8,128)S(1)}, f32[128,384]{0,1:T(8,128)S(1)}, u32[]{:S(2)}, u32[]{:S(2)}) collective-permute-start(f32[128,384]{0,1:T(8,128)S(1)} %slice.336), channel_id=1, source_target_pairs={{0,4},{4,8},{8,12},{12,16},{16,20},{20,24},{24,28},{1,5},{5,9},{9,... | collective-permute-start | bytes 589832 | tf_op jit(solution)/shard_map/ppermute | solution.py:21
  154.7 9.1 %copy-start.17 = (bf16[768,3,192]{0,2,1:T(8,128)(2,1)S(1)}, bf16[768,3,192]{0,2,1:T(8,128)(2,1)}, u32[]{:S(2)}) copy-start(bf16[768,3,192]{0,2,1:T(8,128)(2,1)} %param.25) | copy-start | bytes 2654212
  154.7 8.9 %collective-permute-start.3 = (f32[128,384]{0,1:T(8,128)S(1)}, f32[128,384]{0,1:T(8,128)S(1)}, u32[]{:S(2)}, u32[]{:S(2)}) collective-permute-start(f32[128,384]{0,1:T(8,128)S(1)} %get-tuple-element.59), channel_id=1, source_target_pairs={{4,0},{8,4},{12,8},{16,12},{20,16},{24,20},{28,24},{5,1},{9,5},{13... | collective-permute-start | bytes 589832 | tf_op jit(solution)/shard_map/ppermute | solution.py:23
  167.0 0.9 copy-start.5
  167.0 1.0 copy-start.6
  167.0 182.4 %all-reduce.7.cloned.1.call-start = ((), (), s32[]{:S(2)}) async-start(), calls=%async_computation.2 | async-start | bytes 4718592 | tf_op jit(solution)/shard_map/psum | solution.py:172
  349.4 2.9 copy-start.10
Sparse Core Ops, SparseCore 0:
  167.1 69.0 all-reduce.4
  240.4 108.9 all-reduce.6
where the time goes:
time: 361 us; the launch traced here: 360 us
  waiting for transfers between devices  215 us (60%)
  other arithmetic  33.5 us (9%)
  matrix products  33.5 us (9%)
  local copies, waits for them, and re-layouts  22.3 us (6%)
  blocking collectives  22.3 us (6%)
  starting transfers between devices  19.5 us (5%)
  between operations  14.5 us (4%)
    psum x1, waiting for transfers between devices, per_device(): lax.psum((qkv_part, out_part, gain_part), 'seg')  82.6 us
    psum x1, waiting for transfers between devices, per_device(): grad_hidden = lax.psum(hidden_part, 'mp')  62.2 us
    all_to_all x1, waiting for transfers between devices, per_device(): lax.all_to_all(buffer.reshape(segments, capacity, columns_here), 'seg', s...  59.7 us
    psum x1, blocking collectives, per_device(): lax.psum((qkv_part, out_part, gain_part), 'seg')  22.3 us
    sub x2, matrix products, per_device(): exponent = jnp.where(allowed, jnp.exp(scores - row_top), 0.0)  11.4 us
    gather x2, local copies, waits for them, and re-layouts, per_device(): routed = arrived.reshape(segments * capacity, columns_here)[arrival_slot]  9.59 us
    or x2, other arithmetic, per_device(): allowed = allowed | (listed[:, column:column + 1] == positions[None, :])  9.56 us
    ppermute x2, starting transfers between devices, with_halo(): lax.ppermute(tail, axis, [(i, (i + 1) % count) for i in range(ends)])  9.05 us
  transfers between devices with their start and end apart: 7, of which 6 were waited for; matrix products, arithmetic and copies ran while one was open for 8% of the time, Pallas kernels for 0%

commit v1 on v0

v1 whole, which is shorter than its diff:
```python
import jax
import jax.numpy as jnp
from jax import lax
from jax.experimental import pallas as pl
from jax.experimental.pallas import tpu as pltpu
from jax.sharding import PartitionSpec as P

DH = 64
R = 128
EPSILON = 1e-06
MESH = pl.DeviceIdType.MESH


def exchange(collective_id, *parts):
    arrays = [part[0] for part in parts]
    axes = sorted({part[1] for part in parts})
    counts = {axis: lax.axis_size(axis) for axis in axes}
    shapes = []
    for array, axis, kind in parts:
        lead = (counts[axis],) if kind == "gather" else ()
        shapes.append(jax.ShapeDtypeStruct(lead + array.shape, array.dtype))
    number = len(parts)
    copies = [counts[axis] if kind in ("scatter", "gather") else 1 for _, axis, kind in parts]

    def body(*refs):
        sources, targets = refs[:number], refs[number : 2 * number]
        sends = refs[2 * number : 3 * number]
        receives = refs[3 * number : 4 * number]
        barrier = pltpu.get_barrier_semaphore()
        expected = 0
        for axis in axes:
            here, count = lax.axis_index(axis), counts[axis]
            for step in range(1, count):
                pl.semaphore_signal(
                    barrier,
                    inc=1,
                    device_id={axis: lax.rem(here + step, count)},
                    device_id_type=MESH,
                )
                expected += 1
        pl.semaphore_wait(barrier, expected)
        started = []
        for index, (_, axis, kind) in enumerate(parts):
            source, target = sources[index], targets[index]
            here, count = lax.axis_index(axis), counts[axis]
            if kind in ("next", "prev"):
                step = 1 if kind == "next" else count - 1
                steps = [step]
            else:
                steps = list(range(1, count))
            for slot, step in enumerate(steps):
                peer = lax.rem(here + step, count)
                block = source.at[peer] if kind == "scatter" else source
                place = target if kind in ("next", "prev") else target.at[here]
                copy = pltpu.make_async_remote_copy(
                    src_ref=block,
                    dst_ref=place,
                    send_sem=sends[index].at[slot],
                    recv_sem=receives[index].at[slot],
                    device_id={axis: peer},
                    device_id_type=MESH,
                )
                copy.start()
                started.append(copy)
        for index, (_, axis, kind) in enumerate(parts):
            if kind in ("scatter", "gather"):
                here, count = lax.axis_index(axis), counts[axis]
                source = sources[index]
                block = source.at[here] if kind == "scatter" else source
                own = pltpu.make_async_copy(
                    block, targets[index].at[here], sends[index].at[count - 1]
                )
                own.start()
                started.append(own)
        for copy in started:
            copy.wait()

    return pl.pallas_call(
        body,
        out_shape=shapes,
        in_specs=[pl.BlockSpec(memory_space=pltpu.VMEM)] * number,
        out_specs=[pl.BlockSpec(memory_space=pltpu.VMEM)] * number,
        scratch_shapes=[pltpu.SemaphoreType.DMA((n,)) for n in copies] * 2,
        compiler_params=pltpu.CompilerParams(collective_id=collective_id, has_side_effects=True),
        name=f"exchange_{collective_id}",
    )(*arrays)


def attention(queries, extended, grad_out, neighbours):
    tok_rows, width = queries.shape
    heads = width // DH
    rows = R
    span = rows + 2 * R
    scale = DH ** (-0.5)

    def body(q_ref, kv_ref, g_ref, near_ref, out_ref, dq_ref, grad_ref):
        step = pl.program_id(0)

        @pl.when(step == 0)
        def _():
            grad_ref[...] = jnp.zeros_like(grad_ref)

        start = pl.multiple_of(step * rows, rows)
        first = lax.axis_index("seg") * tok_rows - R + step * rows
        near = near_ref[...] - first
        places = lax.broadcasted_iota(jnp.int32, (rows, span), 1)
        allowed = near[:, 0:1] == places
        for column in range(1, near.shape[1]):
            allowed = allowed | (near[:, column : column + 1] == places)
        window = kv_ref[pl.ds(start, span), :]
        outs, dqs, dks, dvs = [], [], [], []
        for head in range(heads):
            part = slice(head * DH, (head + 1) * DH)
            q, g = q_ref[:, part], g_ref[:, part]
            k = window[:, part]
            v = window[:, width + head * DH : width + (head + 1) * DH]
            across = (((1,), (1,)), ((), ()))
            down = (((0,), (0,)), ((), ()))
            s = lax.dot_general(q, k, across, preferred_element_type=jnp.float32) * scale
            s = jnp.where(allowed, s, -jnp.inf)
            e = jnp.exp(s - jnp.max(s, axis=1, keepdims=True))
            p = e * (1.0 / jnp.sum(e, axis=1, keepdims=True))
            w = p.astype(jnp.bfloat16)
            o = jnp.dot(w, v, preferred_element_type=jnp.float32).astype(jnp.bfloat16)
            delta = jnp.sum(
                g.astype(jnp.float32) * o.astype(jnp.float32), axis=1, keepdims=True
            )
            gp = lax.dot_general(g, v, across, preferred_element_type=jnp.float32)
            ds = (p * (gp - delta) * scale).astype(jnp.bfloat16)
            outs.append(o)
            dqs.append(jnp.dot(ds, k, preferred_element_type=jnp.float32).astype(jnp.bfloat16))
            dks.append(lax.dot_general(ds, q, down, preferred_element_type=jnp.float32))
            dvs.append(lax.dot_general(w, g, down, preferred_element_type=jnp.float32))
        out_ref[...] = jnp.concatenate(outs, axis=1)
        dq_ref[...] = jnp.concatenate(dqs, axis=1)
        grad_ref[pl.ds(start, span), :] += jnp.concatenate(dks + dvs, axis=1)

    by_row = pl.BlockSpec((rows, width), lambda i: (i, 0))
    whole = pl.BlockSpec(extended.shape, lambda i: (0, 0))
    return pl.pallas_call(
        body,
        grid=(tok_rows // rows,),
        in_specs=[
            by_row,
            whole,
            by_row,
            pl.BlockSpec((rows, neighbours.shape[1]), lambda i: (i, 0)),
        ],
        out_specs=[by_row, by_row, whole],
        out_shape=[
            jax.ShapeDtypeStruct((tok_rows, width), jnp.bfloat16),
            jax.ShapeDtypeStruct((tok_rows, width), jnp.bfloat16),
            jax.ShapeDtypeStruct(extended.shape, jnp.float32),
        ],
        name="window_attention",
    )(queries, extended, grad_out, neighbours)


def per_device(
    patches,
    curve_owner,
    arrival_slot,
    patch_level,
    neighbours,
    level_embed,
    norm_gain,
    qkv_weight,
    out_weight,
    cotangent,
):
    segments = lax.axis_size("seg")
    shares = lax.axis_size("mp")
    tok_rows, model_width = patches.shape
    local_width = qkv_weight.shape[2]
    capacity = 2 * tok_rows // segments
    share_width = model_width // shares
    first_column = lax.axis_index("mp") * share_width
    bf16, f32 = jnp.bfloat16, jnp.float32

    def columns_here(array, dim):
        return lax.dynamic_slice_in_dim(array, first_column, share_width, dim)

    row = jnp.arange(tok_rows, dtype=jnp.int32)
    owner_hot = curve_owner[:, None] == jnp.arange(segments, dtype=jnp.int32)[None, :]
    before = (row[None, :] < row[:, None]).astype(bf16)
    counted = jnp.dot(before, owner_hot.astype(bf16), preferred_element_type=f32)
    row_ranks = jnp.sum(jnp.where(owner_hot, counted, 0.0), axis=1).astype(jnp.int32)
    slot_index = curve_owner * capacity + row_ranks
    slots = jnp.arange(segments * capacity, dtype=jnp.int32)
    sent_hot = (slot_index[:, None] == slots[None, :]).astype(bf16)
    packed = lax.dot_general(
        columns_here(patches, 1), sent_hot, (((0,), (0,)), ((), ())), preferred_element_type=f32
    ).astype(bf16)
    packed = packed.reshape(share_width, segments, capacity).transpose(1, 0, 2)
    (arrived,) = exchange(0, (packed, "seg", "scatter"))
    arrived = arrived.transpose(1, 0, 2).reshape(share_width, segments * capacity)
    taken_hot = (slots[:, None] == arrival_slot[None, :]).astype(bf16)
    routed = jnp.dot(arrived, taken_hot, preferred_element_type=f32).astype(bf16)
    (routed,) = exchange(1, (routed, "mp", "gather"))
    routed = routed.reshape(model_width, tok_rows)

    levels = jnp.arange(level_embed.shape[0], dtype=jnp.int32)
    level_hot = (levels[:, None] == patch_level[None, :]).astype(bf16)
    embedded = routed.astype(f32) + lax.dot_general(
        level_embed, level_hot, (((0,), (0,)), ((), ())), preferred_element_type=f32
    )
    inv_rms = lax.rsqrt(jnp.mean(embedded * embedded, axis=0, keepdims=True) + EPSILON)
    normed = embedded * inv_rms
    gain = norm_gain[:, None]
    hidden = (normed * gain).astype(bf16)
    flat_weight = qkv_weight.reshape(model_width, 3 * local_width)
    project = lax.dot_general(
        hidden, flat_weight, (((0,), (0,)), ((), ())), preferred_element_type=f32
    ).astype(bf16)
    queries = project[:, :local_width]
    key_value = project[:, local_width:]
    from_left, from_right = exchange(
        2, (key_value[tok_rows - R :], "seg", "next"), (key_value[:R], "seg", "prev")
    )
    extended = jnp.concatenate([from_left, key_value, from_right], axis=0)
    grad_out = lax.dot_general(
        cotangent, out_weight, (((1,), (1,)), ((), ())), preferred_element_type=f32
    ).astype(bf16)
    attended, grad_query, grad_ext = attention(queries, extended, grad_out, neighbours)
    rim_left, rim_right = exchange(
        3,
        (grad_ext[tok_rows + R :].astype(bf16), "seg", "next"),
        (grad_ext[:R].astype(bf16), "seg", "prev"),
    )
    grad_kv = jnp.concatenate(
        [
            grad_ext[R : 2 * R] + rim_left.astype(f32),
            grad_ext[2 * R : tok_rows],
            grad_ext[tok_rows : tok_rows + R] + rim_right.astype(f32),
        ],
        axis=0,
    )
    grad_qkv = jnp.concatenate([grad_query, grad_kv.astype(bf16)], axis=1)

    qkv_part = lax.dot_general(
        grad_qkv, hidden, (((0,), (1,)), ((), ())), preferred_element_type=f32
    ).astype(bf16)
    out_part = lax.dot_general(
        attended, cotangent, (((0,), (0,)), ((), ())), preferred_element_type=f32
    ).astype(bf16)
    weight_rows = 4 * local_width
    weight_part = jnp.concatenate([qkv_part, out_part], axis=0).reshape(
        segments, weight_rows // segments, model_width
    )
    hidden_part = lax.dot_general(
        flat_weight, grad_qkv, (((1,), (1,)), ((), ())), preferred_element_type=f32
    )
    product = hidden_part * normed
    dots_part = jnp.sum(product * gain, axis=0, keepdims=True)
    gain_part = jnp.sum(product, axis=1).reshape(shares, 1, share_width)
    shared_hidden = hidden_part.astype(bf16).reshape(shares, share_width, tok_rows)
    weights_in, hidden_in, dots_in, gain_in = exchange(
        4,
        (weight_part, "seg", "scatter"),
        (shared_hidden, "mp", "scatter"),
        (dots_part, "mp", "gather"),
        (gain_part, "mp", "scatter"),
    )
    factor = (tok_rows * segments) ** (-0.5)
    weight_sum = (jnp.sum(weights_in.astype(f32), axis=0) * factor).astype(bf16)
    gain_sum = jnp.sum(gain_in, axis=0) * factor
    weights_all, gains_all = exchange(5, (weight_sum, "seg", "gather"), (gain_sum, "seg", "gather"))
    weights_all = weights_all.reshape(weight_rows, model_width).astype(f32)
    qkv_grad = weights_all[: 3 * local_width].T.reshape(model_width, 3, local_width)
    out_grad = weights_all[3 * local_width :]
    gain_grad = jnp.sum(gains_all, axis=0).reshape(share_width)

    grad_hidden = jnp.sum(hidden_in.astype(f32), axis=0)
    mean = jnp.sum(dots_in, axis=0) / model_width
    scaled = grad_hidden * columns_here(gain, 0)
    token_grads = columns_here(cotangent, 1).astype(f32) + (
        inv_rms * (scaled - columns_here(normed, 0) * mean)
    ).T
    return (token_grads, qkv_grad, out_grad, gain_grad)


def solution(mesh):
    placed = (
        P("seg", None),
        P("seg"),
        P("seg"),
        P("seg"),
        P("seg", None),
        P(),
        P(),
        P(None, None, "mp"),
        P("mp", None),
        P("seg", None),
    )
    return jax.shard_map(
        per_device,
        mesh=mesh,
        in_specs=placed,
        out_specs=(P("seg", "mp"), P(None, None, "mp"), P("mp", None), P("mp")),
        check_vma=False,
    )
```

time: 361 us -> 209 us (0.58)
  waiting for transfers between devices: 215 us -> 0 us
  Pallas kernels: 0 us -> 159 us
  blocking collectives: 22.3 us -> 0 us
  starting transfers between devices: 19.5 us -> 0 us
  other arithmetic: 33.5 us -> 16.7 us
  matrix products: 33.5 us -> 19.9 us
  between operations: 14.5 us -> 0.98 us
  local copies, waits for them, and re-layouts: 22.3 us -> 11.9 us
    pallas_call x0 -> x7, Pallas kernels: none -> 159 us  [the longest x6 131 us: exchange(): pl.pallas_call(body, out_shape=shapes, in_specs=[pl.BlockSpec(memory_spac...]
    psum x2 -> x0, waiting for transfers between devices: 145 us -> none  [the longest x1 82.6 us: per_device(): lax.psum((qkv_part, out_part, gain_part), 'seg')]
    all_to_all x1 -> x0, waiting for transfers between devices: 59.7 us -> none  [per_device(): lax.all_to_all(buffer.reshape(segments, capacity, columns_here), 'seg', s...]
    psum x1 -> x0, blocking collectives: 22.3 us -> none  [per_device(): lax.psum((qkv_part, out_part, gain_part), 'seg')]
    ppermute x4 -> x0, starting transfers between devices: 11.8 us -> none  [the longest x2 9.05 us: with_halo(): lax.ppermute(tail, axis, [(i, (i + 1) % count) for i in range(ends)])]
    sub x2 -> x0, matrix products: 11.4 us -> none  [per_device(): exponent = jnp.where(allowed, jnp.exp(scores - row_top), 0.0)]
    ppermute x4 -> x0, waiting for transfers between devices: 10 us -> none  [the longest x2 6.68 us: with_halo(): lax.ppermute(head, axis, [((i + 1) % count, i) for i in range(ends)])]
    gather x2 -> x0, local copies, waits for them, and re-layouts: 9.59 us -> none  [per_device(): routed = arrived.reshape(segments * capacity, columns_here)[arrival_slot]]
  transfers between devices with their start and end apart: 7 -> 0, of which waited for: 6 -> 0; matrix products, arithmetic and copies ran while one was open for 8% -> 0% of each run, Pallas kernels for 0% -> 0%
where the time goes in v1:
time: 209 us; the launch traced here: 208 us
  Pallas kernels  159 us (76%)
  matrix products  19.9 us (10%)
  other arithmetic  16.7 us (8%)
  local copies, waits for them, and re-layouts  11.9 us (6%)
    pallas_call x6, Pallas kernels, exchange(): pl.pallas_call(body, out_shape=shapes, in_specs=[pl.BlockSpec(memory_spac...  131 us
    pallas_call x1, Pallas kernels, attention(): pl.pallas_call(body, grid=(tok_rows // rows,), in_specs=[by_row, whole, b...  27.1 us

profile of v1, /device:TPU:0, one launch (start us, length us, event | category | flops | bytes accessed | tf_op | source)
XLA Modules:
  0.0 208.0 jit_solution(14693480148245178755)
XLA Ops:
  0.6 0.0 copy-start
  0.7 1.3 fusion.10
  2.0 0.7 convert_add_fusion.1
  2.6 3.3 %fusion.5 = bf16[192,2048]{1,0:T(8,128)(2,1)S(1)} fusion(s32[1024]{0:T(1024)S(1)} %convert_add_fusion.1, bf16[1024,768]{1,0:T(8,128)(2,1)} %param.10, s32[]{:T(128)S(6)} %select_n.10), kind=kOutput, calls=%fused_computation.15 | convolution fusion | flops 807796736 | bytes 1314820 | tf_op jit(solution)/shard_map/dot_general | solution.py:191
  6.0 0.0 copy-start.15
  6.0 0.9 copy.41
  6.9 20.8 %exchange_0.1 = bf16[8,192,256]{2,1,0:T(8,128)(2,1)} custom-call(bf16[8,192,256]{2,1,0:T(8,128)(2,1)} %bitcast.49), custom_call_target="tpu_custom_call" | custom-call | tf_op jit(solution)/shard_map/exchange_0/pallas_call | solution.py:78
  27.7 1.2 copy.39
  29.0 2.5 %fusion.8.refs_0_ = bf16[192,1024]{1,0:T(8,128)(2,1)} fusion(bf16[192,2048]{1,0:T(8,128)(2,1)S(1)} %bitcast.54, s32[1024]{0:T(1024)S(1)} %copy-done.15), kind=kOutput, calls=%fused_computation.22 | convolution fusion | flops 807600128 | bytes 1183744 | tf_op jit(solution)/shard_map/dot_general | solution.py:198
  31.5 21.0 %exchange_1.1 = bf16[4,192,1024]{2,1,0:T(8,128)(2,1)} custom-call(bf16[192,1024]{1,0:T(8,128)(2,1)} %fusion.8.refs_0_), custom_call_target="tpu_custom_call" | custom-call | tf_op jit(solution)/shard_map/exchange_1/pallas_call | solution.py:78
  52.6 2.2 %multiply_reduce_fusion.1 = (f32[1024]{0:T(1024)S(1)}, f32[1024,768]{0,1:T(8,128)S(1)}) fusion(bf16[4,192,1024]{2,1,0:T(8,128)(2,1)} %exchange_1.1, bf16[4,768]{1,0:T(4,128)(2,1)S(1)} %copy-done.9, s32[1024]{0:T(1024)S(1)} %copy-done.10), kind=kOutput, calls=%fused_computation.14 | convolution fusion | flops 9440256 | bytes 4732928 | tf_op jit(solution)/shard_map/dot_general | solution.py:204
  54.8 0.9 fusion.6
  55.7 0.3 copy-done.11
  56.0 1.7 convolution_convert_fusion
  57.6 0.8 fusion.19
  58.4 16.3 %exchange_2.1 = (bf16[128,384]{1,0:T(8,128)(2,1)}, bf16[128,384]{1,0:T(8,128)(2,1)}) custom-call(bf16[128,384]{1,0:T(8,128)(2,1)} %get-tuple-element.35.refs_0_, bf16[128,384]{1,0:T(8,128)(2,1)} %get-tuple-element.34.refs_1_), custom_call_target="tpu_custom_call" | custom-call | tf_op jit(solution)/shard_map/exchange_2/pallas_call | solution.py:78
  74.8 0.3 slice.60
  75.1 2.0 pad_maximum_fusion.1.kv_ref
  77.1 0.8 slice.57.q_ref
  77.9 0.7 convolution_convert_fusion.2
  78.6 1.0 copy.34.g_ref
  79.6 1.0 copy.35.near_ref
  80.6 27.1 %window_attention.1 = (bf16[1024,192]{1,0:T(8,128)(2,1)}, bf16[1024,192]{1,0:T(8,128)(2,1)}, f32[1280,384]{1,0:T(8,128)}) custom-call(bf16[1024,192]{1,0:T(8,128)(2,1)} %slice.57.q_ref, bf16[1280,384]{1,0:T(8,128)(2,1)} %pad_maximum_fusion.1.kv_ref, bf16[1024,192]{1,0:T(8,128)(2,1)} %copy.34.g_ref, s32[1024,16]{1,0:T(8,128)} %copy.35.near_ref), custom_call_target="tpu_custom_call" | custom-call | tf_op jit(solution)/shard_map/window_attention/pallas_call | solution.py:140
  107.8 1.7 convert.13
  109.4 0.7 fusion.20
  110.1 9.1 %exchange_3.1 = (bf16[128,384]{1,0:T(8,128)(2,1)}, bf16[128,384]{1,0:T(8,128)(2,1)}) custom-call(bf16[128,384]{1,0:T(8,128)(2,1)} %get-tuple-element.37.refs_0_, bf16[128,384]{1,0:T(8,128)(2,1)} %get-tuple-element.36.refs_1_), custom_call_target="tpu_custom_call" | custom-call | tf_op jit(solution)/shard_map/exchange_3/pallas_call | solution.py:78
  119.2 1.2 add_convert_fusion.1
  120.4 0.1 slice.63
  120.5 4.1 %bitcast_convert_fusion = (bf16[768,1024]{1,0:T(8,128)(2,1)}, f32[1024,768]{0,1:T(8,128)S(1)}) fusion(bf16[768,576]{0,1:T(8,128)(2,1)} %bitcast.58, bf16[128,384]{1,0:T(8,128)(2,1)S(1)} %get-tuple-element.33, bf16[768,384]{1,0:T(8,128)(2,1)S(1)} %slice.63, bf16[128,384]{1,0:T(8,128)(2,1)S(1)} %get-tuple-element.32, bf16[1024,192]{1,0:T(8,128)(2,1)} %get-tuple-element.19), kind=kOutput, calls=%fused_computation.10 | convolution fusion | flops 911474688 | bytes 6782976 | tf_op jit(solution)/shard_map/dot_general | solution.py:250
  124.6 1.2 fusion.7
  125.8 0.7 reshape.75.refs_3_
  126.4 3.6 %convolution_convert_fusion.1 = bf16[576,768]{1,0:T(8,128)(2,1)S(1)} fusion(bf16[128,384]{1,0:T(8,128)(2,1)S(1)} %get-tuple-element.33, bf16[768,384]{1,0:T(8,128)(2,1)S(1)} %slice.63, bf16[128,384]{1,0:T(8,128)(2,1)S(1)} %get-tuple-element.32, bf16[1024,192]{1,0:T(8,128)(2,1)S(1)} %copy-done.13, f32[768,1024]{1,0:T(8,128)} %copy-done.1, f32[768]{0:T(1024)S(1)} %copy-done.8), kind=kOutput, calls=%fused_computation.19 | convolution fusion | flops 912703488 | bytes 5213184 | tf_op jit(solution)/shard_map/dot_general | solution.py:240
  130.1 0.5 convolution_convert_fusion.3
  130.6 1.1 pad_maximum_fusion
  131.7 25.8 %exchange_4.1 = (bf16[8,96,768]{2,1,0:T(8,128)(2,1)}, bf16[4,192,1024]{2,1,0:T(8,128)(2,1)}, f32[4,1,1024]{2,1,0:T(1,128)}, f32[4,1,192]{2,1,0:T(1,128)}) custom-call(bf16[8,96,768]{2,1,0:T(8,128)(2,1)} %bitcast.48, bf16[4,192,1024]{2,1,0:T(8,128)(2,1)} %bitcast.52, f32[1,1024]{1,0:T(1,128)} %bitcast.56, f32[4,1,192]{2,1,0:T(1,128)} %reshape.75.refs_3_), custom_call_target="tpu_custom_call" | custom-call | tf_op jit(solution)/shard_map/exchange_4/pallas_call | solution.py:78
  157.5 1.5 convert_reduce_fusion.1
  159.0 0.7 multiply_convert_fusion.1.refs_0_
  159.7 0.7 reduce_sum.88
  160.4 0.6 broadcast_multiply_fusion.1
  160.9 38.4 %exchange_5.1 = (bf16[8,96,768]{2,1,0:T(8,128)(2,1)}, f32[8,1,192]{2,1,0:T(1,128)}) custom-call(bf16[96,768]{1,0:T(8,128)(2,1)} %multiply_convert_fusion.1.refs_0_, f32[1,192]{1,0:T(1,128)} %bitcast.57), custom_call_target="tpu_custom_call" | custom-call | tf_op jit(solution)/shard_map/exchange_5/pallas_call | solution.py:78
  199.3 2.6 %slice.64 = f32[6,96,768]{2,1,0:T(8,128)} slice(bf16[8,96,768]{2,1,0:T(8,128)(2,1)} %get-tuple-element.28), slice={[0:6], [0:96], [0:768]} | slice | bytes 3538944 | tf_op jit(solution)/shard_map/slice | solution.py:269
  202.0 0.9 slice.65
  202.8 0.6 reduce_sum.89
  203.4 1.8 convert_reduce_fusion
  205.2 0.2 constant_dynamic-slice_fusion
  205.5 0.2 copy.37
  205.7 0.1 dynamic-slice.3
  205.8 2.2 %bitcast_add_fusion = f32[1024,192]{0,1:T(8,128)} fusion(f32[768,1024]{1,0:T(8,128)} %copy-done.1, s32[]{:T(128)S(6)} %select_n.10, f32[192,1024]{1,0:T(8,128)S(1)} %convert_reduce_fusion, bf16[1024,192]{0,1:T(8,128)(2,1)S(1)} %copy.37, f32[1024]{0:T(1024)S(1)} %broadcast_multiply_fusion, f32[192]{0:T(256)S(1)} %dynamic-slice.3, f32[1024]{0:T(1024)S(1)} %add_rsqrt_fusion), kind=kLoop, calls=%fused_computation.30 | loop fusion | flops 1179648 | bytes 2761476 | tf_op jit(solution)/shard_map/add | solution.py:276
  (32 shorter events, 0.1 us)
Async XLA Ops:
  0.6 77.3 %copy-start = (bf16[1024,768]{1,0:T(8,128)(2,1)S(1)}, bf16[1024,768]{1,0:T(8,128)(2,1)}, u32[]{:S(2)}) copy-start(bf16[1024,768]{1,0:T(8,128)(2,1)} %param.19) | copy-start | bytes 4718596
  6.0 23.0 %copy-start.15 = (s32[1024]{0:T(1024)S(1)}, s32[1024]{0:T(1024)}, u32[]{:S(2)}) copy-start(s32[1024]{0:T(1024)} %param.12) | copy-start | bytes 12292
  29.0 23.6 %copy-start.9 = (bf16[4,768]{1,0:T(4,128)(2,1)S(1)}, bf16[4,768]{1,0:T(4,128)(2,1)}, u32[]{:S(2)}) copy-start(bf16[4,768]{1,0:T(4,128)(2,1)} %param.15) | copy-start | bytes 18436
  29.0 23.6 %copy-start.10 = (s32[1024]{0:T(1024)S(1)}, s32[1024]{0:T(1024)}, u32[]{:S(2)}) copy-start(s32[1024]{0:T(1024)} %param.13) | copy-start | bytes 12292
  52.5 2.2 %copy-start.3 = (bf16[4,192,1024]{2,1,0:T(8,128)(2,1)S(1)}, bf16[4,192,1024]{2,1,0:T(8,128)(2,1)}, u32[]{:S(2)}) copy-start(bf16[4,192,1024]{2,1,0:T(8,128)(2,1)} %exchange_1.1) | copy-start | bytes 4718596
  54.8 0.9 copy-start.8
  54.8 1.2 copy-start.11
  55.7 1.9 copy-start.1
  74.8 3.2 %copy-start.14 = (bf16[192,768]{1,0:T(8,128)(2,1)S(1)}, bf16[192,768]{1,0:T(8,128)(2,1)}, u32[]{:S(2)}) copy-start(bf16[192,768]{1,0:T(8,128)(2,1)} %param.18) | copy-start | bytes 884740
  77.1 2.5 %copy-start.5 = (s32[1024,16]{0,1:T(8,128)S(1)}, s32[1024,16]{0,1:T(8,128)}, u32[]{:S(2)}) copy-start(s32[1024,16]{0,1:T(8,128)} %param.14) | copy-start | bytes 196612
  120.4 4.1 %copy-start.2 = (f32[768,1024]{1,0:T(8,128)S(1)}, f32[768,1024]{1,0:T(8,128)}, u32[]{:S(2)}) copy-start(f32[768,1024]{1,0:T(8,128)} %copy-done.1) | copy-start | bytes 9437188
  124.6 1.8 copy-start.13
  126.4 3.6 %copy-start.12 = (bf16[1024,192]{1,0:T(8,128)(2,1)S(1)}, bf16[1024,192]{1,0:T(8,128)(2,1)}, u32[]{:S(2)}) copy-start(bf16[1024,192]{1,0:T(8,128)(2,1)} %get-tuple-element.23) | copy-start | bytes 1179652
  199.3 2.6 %copy-start.4 = (bf16[8,96,768]{2,1,0:T(8,128)(2,1)S(1)}, bf16[8,96,768]{2,1,0:T(8,128)(2,1)}, u32[]{:S(2)}) copy-start(bf16[8,96,768]{2,1,0:T(8,128)(2,1)} %get-tuple-element.28) | copy-start | bytes 3538948
  199.3 3.5 %copy-start.7 = (f32[8,1,192]{2,1,0:T(1,128)S(1)}, f32[8,1,192]{2,1,0:T(1,128)}, u32[]{:S(2)}) copy-start(f32[8,1,192]{2,1,0:T(1,128)} %get-tuple-element.29) | copy-start | bytes 18436
  202.0 3.2 %copy-start.6 = (f32[4,1,1024]{2,1,0:T(1,128)S(1)}, f32[4,1,1024]{2,1,0:T(1,128)}, u32[]{:S(2)}) copy-start(f32[4,1,1024]{2,1,0:T(1,128)} %get-tuple-element.25) | copy-start | bytes 49156

commit v2 on v1

--- a/solution.py
+++ b/solution.py
@@ -15,17 +15,119 @@
     arrays = [part[0] for part in parts]
     axes = sorted({part[1] for part in parts})
     counts = {axis: lax.axis_size(axis) for axis in axes}
-    shapes = []
+    shapes, slots = [], []
     for array, axis, kind in parts:
-        lead = (counts[axis],) if kind == "gather" else ()
+        count = counts[axis]
+        lead = (count,) if kind in ("gather", "direct") else ()
         shapes.append(jax.ShapeDtypeStruct(lead + array.shape, array.dtype))
+        slots.append({"scatter": count, "direct": count, "gather": 2 * count}.get(kind, 1))
     number = len(parts)
-    copies = [counts[axis] if kind in ("scatter", "gather") else 1 for _, axis, kind in parts]
+
+    def remote(source, target, sends, receives, slot, axis, peer):
+        return pltpu.make_async_remote_copy(
+            src_ref=source,
+            dst_ref=target,
+            send_sem=sends.at[slot],
+            recv_sem=receives.at[slot],
+            device_id={axis: peer},
+            device_id_type=MESH,
+        )
+
+    def scatter(source, target, sends, receives, axis, split):
+        here, count = lax.axis_index(axis), counts[axis]
+        copies = []
+        for step in range(1, count):
+            peer = lax.rem(here + step, count)
+            block = source.at[peer] if split else source
+            copies.append(remote(block, target.at[here], sends, receives, step, axis, peer))
+        block = source.at[here] if split else source
+        copies.append(pltpu.make_async_copy(block, target.at[here], sends.at[0]))
+        for copy in copies:
+            copy.start()
+
+        def finish():
+            for copy in copies:
+                copy.wait()
+
+        return (lambda: None), finish
+
+    def shift(source, target, sends, receives, axis, forward):
+        here, count = lax.axis_index(axis), counts[axis]
+        step = 1 if forward else -1
+        peer = lax.rem(here + step + count, count)
+        has_peer = here < count - 1 if forward else here > 0
+        has_source = here > 0 if forward else here < count - 1
+        copy = remote(source, target, sends, receives, 0, axis, peer)
+        pl.when(has_peer)(copy.start)
+
+        def finish():
+            pl.when(has_peer)(copy.wait_send)
+            pl.when(has_source)(copy.wait_recv)
+
+        return (lambda: None), finish
+
+    def gather(source, target, sends, receives, axis):
+        here, count = lax.axis_index(axis), counts[axis]
+        line = count // 2
+        outer = here // 2
+        partner = here + 1 - 2 * lax.rem(here, 2)
+        ahead = lax.rem(here + 2, count)
+        behind = lax.rem(here + count - 2, count)
+        own = pltpu.make_async_copy(source, target.at[here], sends.at[0])
+
+        def block(shift):
+            return target.at[lax.rem(here + 2 * shift + count, count)]
+
+        def hand_on(shift, direction, step):
+            peer = ahead if direction > 0 else behind
+            slot = step if direction > 0 else line + step
+            taken = source if shift == 0 else block(shift)
+            return remote(taken, block(shift), sends, receives, slot, axis, peer)
+
+        def hand_over(shift):
+            slot = 2 * line + (shift if shift >= 0 else line - 1 - shift)
+            taken = source if shift == 0 else block(shift)
+            return remote(taken, block(shift), sends, receives, slot, axis, partner)
+
+        def there(shift):
+            place = outer + shift
+            return (place >= 0) if shift < 0 else (place < line)
+
+        if line > 1:
+            pl.when(there(1))(hand_on(0, 1, 1).start)
+            pl.when(there(-1))(hand_on(0, -1, 1).start)
+        hand_over(0).start()
+        own.start()
+
+        def relay():
+            for step in range(1, line):
+                for direction in (1, -1):
+                    came = -direction * step
+
+                    @pl.when(there(came))
+                    def _():
+                        hand_on(came, direction, step).wait_recv()
+                        if step < line - 1:
+                            pl.when(there(direction))(hand_on(came, direction, step + 1).start)
+                        hand_over(came).start()
+
+        def finish():
+            for step in range(1, line):
+                for direction in (1, -1):
+                    came = -direction * (step - 1)
+
+                    @pl.when(there(direction) if step == 1 else there(came) & there(direction))
+                    def _():
+                        hand_on(came, direction, step).wait_send()
+
+                    pl.when(there(direction * step))(hand_over(direction * step).wait)
+            hand_over(0).wait()
+            own.wait()
+
+        return relay, finish
 
     def body(*refs):
-        sources, targets = refs[:number], refs[number : 2 * number]
-        sends = refs[2 * number : 3 * number]
-        receives = refs[3 * number : 4 * number]
+        groups = [refs[i * number : (i + 1) * number] for i in range(4)]
         barrier = pltpu.get_barrier_semaphore()
         expected = 0
         for axis in axes:
@@ -39,48 +141,25 @@
                 )
                 expected += 1
         pl.semaphore_wait(barrier, expected)
-        started = []
-        for index, (_, axis, kind) in enumerate(parts):
-            source, target = sources[index], targets[index]
-            here, count = lax.axis_index(axis), counts[axis]
-            if kind in ("next", "prev"):
-                step = 1 if kind == "next" else count - 1
-                steps = [step]
+        pending = []
+        for (_, axis, kind), *held in zip(parts, *groups):
+            if kind in ("scatter", "direct"):
+                pending.append(scatter(*held, axis, kind == "scatter"))
+            elif kind == "gather":
+                pending.append(gather(*held, axis))
             else:
-                steps = list(range(1, count))
-            for slot, step in enumerate(steps):
-                peer = lax.rem(here + step, count)
-                block = source.at[peer] if kind == "scatter" else source
-                place = target if kind in ("next", "prev") else target.at[here]
-                copy = pltpu.make_async_remote_copy(
-                    src_ref=block,
-                    dst_ref=place,
-                    send_sem=sends[index].at[slot],
-                    recv_sem=receives[index].at[slot],
-                    device_id={axis: peer},
-                    device_id_type=MESH,
-                )
-                copy.start()
-                started.append(copy)
-        for index, (_, axis, kind) in enumerate(parts):
-            if kind in ("scatter", "gather"):
-                here, count = lax.axis_index(axis), counts[axis]
-                source = sources[index]
-                block = source.at[here] if kind == "scatter" else source
-                own = pltpu.make_async_copy(
-                    block, targets[index].at[here], sends[index].at[count - 1]
-                )
-                own.start()
-                started.append(own)
-        for copy in started:
-            copy.wait()
+                pending.append(shift(*held, axis, kind == "next"))
+        for relay, _ in pending:
+            relay()
+        for _, finish in pending:
+            finish()
 
     return pl.pallas_call(
         body,
         out_shape=shapes,
         in_specs=[pl.BlockSpec(memory_space=pltpu.VMEM)] * number,
         out_specs=[pl.BlockSpec(memory_space=pltpu.VMEM)] * number,
-        scratch_shapes=[pltpu.SemaphoreType.DMA((n,)) for n in copies] * 2,
+        scratch_shapes=[pltpu.SemaphoreType.DMA((n,)) for n in slots] * 2,
         compiler_params=pltpu.CompilerParams(collective_id=collective_id, has_side_effects=True),
         name=f"exchange_{collective_id}",
     )(*arrays)
@@ -217,6 +296,9 @@
     from_left, from_right = exchange(
         2, (key_value[tok_rows - R :], "seg", "next"), (key_value[:R], "seg", "prev")
     )
+    segment = lax.axis_index("seg")
+    from_left = jnp.where(segment > 0, from_left, 0)
+    from_right = jnp.where(segment < segments - 1, from_right, 0)
     extended = jnp.concatenate([from_left, key_value, from_right], axis=0)
     grad_out = lax.dot_general(
         cotangent, out_weight, (((1,), (1,)), ((), ())), preferred_element_type=f32
@@ -227,6 +309,8 @@
         (grad_ext[tok_rows + R :].astype(bf16), "seg", "next"),
         (grad_ext[:R].astype(bf16), "seg", "prev"),
     )
+    rim_left = jnp.where(segment > 0, rim_left, 0)
+    rim_right = jnp.where(segment < segments - 1, rim_right, 0)
     grad_kv = jnp.concatenate(
         [
             grad_ext[R : 2 * R] + rim_left.astype(f32),
@@ -254,17 +338,17 @@
     dots_part = jnp.sum(product * gain, axis=0, keepdims=True)
     gain_part = jnp.sum(product, axis=1).reshape(shares, 1, share_width)
     shared_hidden = hidden_part.astype(bf16).reshape(shares, share_width, tok_rows)
-    weights_in, hidden_in, dots_in, gain_in = exchange(
+    dots_in, gain_in, weights_in, hidden_in = exchange(
         4,
+        (dots_part, "mp", "direct"),
+        (gain_part, "mp", "scatter"),
         (weight_part, "seg", "scatter"),
         (shared_hidden, "mp", "scatter"),
-        (dots_part, "mp", "gather"),
-        (gain_part, "mp", "scatter"),
     )
     factor = (tok_rows * segments) ** (-0.5)
     weight_sum = (jnp.sum(weights_in.astype(f32), axis=0) * factor).astype(bf16)
     gain_sum = jnp.sum(gain_in, axis=0) * factor
-    weights_all, gains_all = exchange(5, (weight_sum, "seg", "gather"), (gain_sum, "seg", "gather"))
+    gains_all, weights_all = exchange(5, (gain_sum, "seg", "direct"), (weight_sum, "seg", "gather"))
     weights_all = weights_all.reshape(weight_rows, model_width).astype(f32)
     qkv_grad = weights_all[: 3 * local_width].T.reshape(model_width, 3, local_width)
     out_grad = weights_all[3 * local_width :]

time: 209 us -> 192 us (0.919)
  Pallas kernels: 159 us -> 142 us
    pallas_call x6, Pallas kernels: 131 us -> 115 us  [exchange(): pl.pallas_call(body, out_shape=shapes, in_specs=[pl.BlockSpec(memory_spac...]
where the time goes in v2:
time: 192 us; the launch traced here: 191 us
  Pallas kernels  142 us (74%)
  matrix products  19.2 us (10%)
  other arithmetic  15.6 us (8%)
  local copies, waits for them, and re-layouts  12.7 us (7%)
    pallas_call x6, Pallas kernels, exchange(): pl.pallas_call(body, out_shape=shapes, in_specs=[pl.BlockSpec(memory_spac...  115 us
    pallas_call x1, Pallas kernels, attention(): pl.pallas_call(body, grid=(tok_rows // rows,), in_specs=[by_row, whole, b...  27.1 us

profile of v2, /device:TPU:0, one launch (start us, length us, event | category | flops | bytes accessed | tf_op | source)
XLA Modules:
  0.0 190.9 jit_solution(8462562425503246875)
XLA Ops:
  0.7 1.3 fusion.10
  2.0 0.7 convert_add_fusion.1
  2.6 3.3 %fusion.5 = bf16[192,2048]{1,0:T(8,128)(2,1)S(1)} fusion(s32[1024]{0:T(1024)S(1)} %convert_add_fusion.1, bf16[1024,768]{1,0:T(8,128)(2,1)} %param.10, s32[]{:T(128)S(6)} %select_n.32), kind=kOutput, calls=%fused_computation.15 | convolution fusion | flops 807796736 | bytes 1314820 | tf_op jit(solution)/shard_map/dot_general | solution.py:270
  6.0 0.9 copy.41
  6.9 20.8 %exchange_0.1 = bf16[8,192,256]{2,1,0:T(8,128)(2,1)} custom-call(bf16[8,192,256]{2,1,0:T(8,128)(2,1)} %bitcast.50), custom_call_target="tpu_custom_call" | custom-call | tf_op jit(solution)/shard_map/exchange_0/pallas_call | solution.py:157
  27.7 1.2 copy.39
  29.0 2.5 %fusion.8.refs_0_ = bf16[192,1024]{1,0:T(8,128)(2,1)} fusion(bf16[192,2048]{1,0:T(8,128)(2,1)S(1)} %bitcast.55, s32[1024]{0:T(1024)S(1)} %copy-done.16), kind=kOutput, calls=%fused_computation.22 | convolution fusion | flops 807600128 | bytes 1183744 | tf_op jit(solution)/shard_map/dot_general | solution.py:277
  31.5 15.1 %exchange_1.1 = bf16[4,192,1024]{2,1,0:T(8,128)(2,1)} custom-call(bf16[192,1024]{1,0:T(8,128)(2,1)} %fusion.8.refs_0_), custom_call_target="tpu_custom_call" | custom-call | tf_op jit(solution)/shard_map/exchange_1/pallas_call | solution.py:157
  46.6 2.2 %multiply_reduce_fusion.1 = (f32[1024]{0:T(1024)S(1)}, f32[1024,768]{0,1:T(8,128)S(1)}) fusion(bf16[4,192,1024]{2,1,0:T(8,128)(2,1)} %exchange_1.1, bf16[4,768]{1,0:T(4,128)(2,1)S(1)} %copy-done.8, s32[1024]{0:T(1024)S(1)} %copy-done.9), kind=kOutput, calls=%fused_computation.14 | convolution fusion | flops 9440256 | bytes 4732928 | tf_op jit(solution)/shard_map/dot_general | solution.py:283
  48.8 0.9 fusion.6
  49.7 0.3 copy-done.11
  50.0 1.7 convolution_convert_fusion
  51.7 0.8 fusion.19
  52.5 14.8 %exchange_2.1 = (bf16[128,384]{1,0:T(8,128)(2,1)}, bf16[128,384]{1,0:T(8,128)(2,1)}) custom-call(bf16[128,384]{1,0:T(8,128)(2,1)} %get-tuple-element.35.refs_0_, bf16[128,384]{1,0:T(8,128)(2,1)} %get-tuple-element.34.refs_1_), custom_call_target="tpu_custom_call" | custom-call | tf_op jit(solution)/shard_map/exchange_2/pallas_call | solution.py:157
  67.3 0.9 broadcast_select_fusion
  68.2 0.3 slice.60
  68.6 1.0 pad_maximum_fusion.1.kv_ref
  69.6 0.8 slice.57.q_ref
  70.4 0.7 convolution_convert_fusion.2
  71.1 1.0 copy.34.g_ref
  72.1 1.0 copy.35.near_ref
  73.1 27.1 %window_attention.1 = (bf16[1024,192]{1,0:T(8,128)(2,1)}, bf16[1024,192]{1,0:T(8,128)(2,1)}, f32[1280,384]{1,0:T(8,128)}) custom-call(bf16[1024,192]{1,0:T(8,128)(2,1)} %slice.57.q_ref, bf16[1280,384]{1,0:T(8,128)(2,1)} %pad_maximum_fusion.1.kv_ref, bf16[1024,192]{1,0:T(8,128)(2,1)} %copy.34.g_ref, s32[1024,16]{1,0:T(8,128)} %copy.35.near_ref), custom_call_target="tpu_custom_call" | custom-call | tf_op jit(solution)/shard_map/window_attention/pallas_call | solution.py:219
  100.3 1.7 convert.13
  102.0 0.7 fusion.20
  102.7 8.5 %exchange_3.1 = (bf16[128,384]{1,0:T(8,128)(2,1)}, bf16[128,384]{1,0:T(8,128)(2,1)}) custom-call(bf16[128,384]{1,0:T(8,128)(2,1)} %get-tuple-element.37.refs_0_, bf16[128,384]{1,0:T(8,128)(2,1)} %get-tuple-element.36.refs_1_), custom_call_target="tpu_custom_call" | custom-call | tf_op jit(solution)/shard_map/exchange_3/pallas_call | solution.py:157
  111.2 1.1 add_convert_fusion.1
  112.4 0.1 slice.63
  112.4 3.6 %convolution_convert_fusion.1 = bf16[576,768]{1,0:T(8,128)(2,1)S(1)} fusion(bf16[128,384]{1,0:T(8,128)(2,1)S(1)} %get-tuple-element.33, bf16[768,384]{1,0:T(8,128)(2,1)S(1)} %slice.63, bf16[128,384]{1,0:T(8,128)(2,1)S(1)} %get-tuple-element.32, bf16[1024,192]{1,0:T(8,128)(2,1)S(1)} %copy-done.13, f32[768,1024]{1,0:T(8,128)} %copy-done.2, f32[768]{0:T(1024)S(1)} %copy-done.10), kind=kOutput, calls=%fused_computation.19 | convolution fusion | flops 912703488 | bytes 5213184 | tf_op jit(solution)/shard_map/dot_general | solution.py:324
  116.1 0.5 convolution_convert_fusion.3
  116.6 1.1 pad_maximum_fusion
  117.7 0.6 copy-done.3
  118.4 0.2 copy-done.12
  118.6 3.4 %fusion.7 = (f32[768]{0:T(1024)S(1)}, f32[1024]{0:T(1024)}, bf16[1024,768]{0,1:T(8,128)(2,1)}) fusion(f32[768,1024]{1,0:T(8,128)S(1)} %copy-done.3, f32[768]{0:T(1024)S(1)} %copy-done.10, bf16[768,576]{0,1:T(8,128)(2,1)S(1)} %bitcast.60, bf16[128,384]{1,0:T(8,128)(2,1)S(1)} %get-tuple-element.33, bf16[768,384]{1,0:T(8,128)(2,1)S(1)} %slice.63, ...), kind=kOutput, calls=%fused_computation.20 | convolution fusion | flops 914618624 | bytes 6793216 | tf_op jit(solution)/shard_map/dot_general | solution.py:334
  122.0 0.7 reshape.73.refs_1_
  122.7 27.2 %exchange_4.1 = (f32[4,1,1024]{2,1,0:T(1,128)}, f32[4,1,192]{2,1,0:T(1,128)}, bf16[8,96,768]{2,1,0:T(8,128)(2,1)}, bf16[4,192,1024]{2,1,0:T(8,128)(2,1)}) custom-call(f32[1,1024]{1,0:T(1,128)} %bitcast.57, f32[4,1,192]{2,1,0:T(1,128)} %reshape.73.refs_1_, bf16[8,96,768]{2,1,0:T(8,128)(2,1)} %bitcast.49, bf16[4,192,1024]{2,1,0:T(8,128)(2,1)} %bitcast.53), custom_call_target="tpu_custom_call" | custom-call | tf_op jit(solution)/shard_map/exchange_4/pallas_call | solution.py:157
  149.9 1.5 convert_reduce_fusion.1
  151.4 0.7 multiply_convert_fusion.1.refs_1_
  152.0 0.7 reduce_sum.87
  152.7 0.6 broadcast_multiply_fusion.1
  153.3 28.9 %exchange_5.1 = (f32[8,1,192]{2,1,0:T(1,128)}, bf16[8,96,768]{2,1,0:T(8,128)(2,1)}) custom-call(f32[1,192]{1,0:T(1,128)} %bitcast.58, bf16[96,768]{1,0:T(8,128)(2,1)} %multiply_convert_fusion.1.refs_1_), custom_call_target="tpu_custom_call" | custom-call | tf_op jit(solution)/shard_map/exchange_5/pallas_call | solution.py:157
  182.2 2.6 %slice.64 = f32[6,96,768]{2,1,0:T(8,128)} slice(bf16[8,96,768]{2,1,0:T(8,128)(2,1)} %get-tuple-element.28), slice={[0:6], [0:96], [0:768]} | slice | bytes 3538944 | tf_op jit(solution)/shard_map/slice | solution.py:353
  184.9 0.9 slice.65
  185.7 0.6 reduce_sum.89
  186.3 1.8 convert_reduce_fusion
  188.1 0.2 constant_dynamic-slice_fusion
  188.4 0.2 copy.37
  188.6 0.1 dynamic-slice.3
  188.6 2.2 %bitcast_add_fusion = f32[1024,192]{0,1:T(8,128)} fusion(f32[768,1024]{1,0:T(8,128)} %copy-done.2, s32[]{:T(128)S(6)} %select_n.32, f32[192,1024]{1,0:T(8,128)S(1)} %convert_reduce_fusion, bf16[1024,192]{0,1:T(8,128)(2,1)S(1)} %copy.37, f32[1024]{0:T(1024)S(1)} %broadcast_multiply_fusion, f32[192]{0:T(256)S(1)} %dynamic-slice.3, f32[1024]{0:T(1024)S(1)} %add_rsqrt_fusion), kind=kLoop, calls=%fused_computation.30 | loop fusion | flops 1179648 | bytes 2761476 | tf_op jit(solution)/shard_map/add | solution.py:360
  (34 shorter events, 0.1 us)
Async XLA Ops:
  0.6 69.8 %copy-start = (bf16[1024,768]{1,0:T(8,128)(2,1)S(1)}, bf16[1024,768]{1,0:T(8,128)(2,1)}, u32[]{:S(2)}) copy-start(bf16[1024,768]{1,0:T(8,128)(2,1)} %param.19) | copy-start | bytes 4718596
  6.0 23.0 %copy-start.16 = (s32[1024]{0:T(1024)S(1)}, s32[1024]{0:T(1024)}, u32[]{:S(2)}) copy-start(s32[1024]{0:T(1024)} %param.12) | copy-start | bytes 12292
  29.0 17.6 %copy-start.8 = (bf16[4,768]{1,0:T(4,128)(2,1)S(1)}, bf16[4,768]{1,0:T(4,128)(2,1)}, u32[]{:S(2)}) copy-start(bf16[4,768]{1,0:T(4,128)(2,1)} %param.15) | copy-start | bytes 18436
  29.0 17.6 %copy-start.9 = (s32[1024]{0:T(1024)S(1)}, s32[1024]{0:T(1024)}, u32[]{:S(2)}) copy-start(s32[1024]{0:T(1024)} %param.13) | copy-start | bytes 12292
  46.6 2.2 %copy-start.1 = (bf16[4,192,1024]{2,1,0:T(8,128)(2,1)S(1)}, bf16[4,192,1024]{2,1,0:T(8,128)(2,1)}, u32[]{:S(2)}) copy-start(bf16[4,192,1024]{2,1,0:T(8,128)(2,1)} %exchange_1.1) | copy-start | bytes 4718596
  48.8 0.9 copy-start.10
  48.8 1.2 copy-start.11
  49.7 1.9 %copy-start.2 = (f32[768,1024]{1,0:T(8,128)}, f32[768,1024]{1,0:T(8,128)S(1)}, u32[]{:S(2)}) copy-start(f32[768,1024]{1,0:T(8,128)S(1)} %fusion.6) | copy-start | bytes 9437188
  68.2 2.2 %copy-start.15 = (bf16[192,768]{1,0:T(8,128)(2,1)S(1)}, bf16[192,768]{1,0:T(8,128)(2,1)}, u32[]{:S(2)}) copy-start(bf16[192,768]{1,0:T(8,128)(2,1)} %param.18) | copy-start | bytes 884740
  69.6 2.5 %copy-start.5 = (s32[1024,16]{0,1:T(8,128)S(1)}, s32[1024,16]{0,1:T(8,128)}, u32[]{:S(2)}) copy-start(s32[1024,16]{0,1:T(8,128)} %param.14) | copy-start | bytes 196612
  100.3 12.2 %copy-start.13 = (bf16[1024,192]{1,0:T(8,128)(2,1)S(1)}, bf16[1024,192]{1,0:T(8,128)(2,1)}, u32[]{:S(2)}) copy-start(bf16[1024,192]{1,0:T(8,128)(2,1)} %get-tuple-element.19) | copy-start | bytes 1179652
  112.4 3.6 %copy-start.14 = (bf16[1024,192]{1,0:T(8,128)(2,1)S(1)}, bf16[1024,192]{1,0:T(8,128)(2,1)}, u32[]{:S(2)}) copy-start(bf16[1024,192]{1,0:T(8,128)(2,1)} %get-tuple-element.23) | copy-start | bytes 1179652
  116.1 2.3 %copy-start.3 = (f32[768,1024]{1,0:T(8,128)S(1)}, f32[768,1024]{1,0:T(8,128)}, u32[]{:S(2)}) copy-start(f32[768,1024]{1,0:T(8,128)} %copy-done.2) | copy-start | bytes 9437188
  116.1 2.5 %copy-start.12 = (bf16[768,3,192]{0,2,1:T(8,128)(2,1)S(1)}, bf16[768,3,192]{0,2,1:T(8,128)(2,1)}, u32[]{:S(2)}) copy-start(bf16[768,3,192]{0,2,1:T(8,128)(2,1)} %param.17) | copy-start | bytes 2654212
  182.2 2.6 %copy-start.4 = (bf16[8,96,768]{2,1,0:T(8,128)(2,1)S(1)}, bf16[8,96,768]{2,1,0:T(8,128)(2,1)}, u32[]{:S(2)}) copy-start(bf16[8,96,768]{2,1,0:T(8,128)(2,1)} %get-tuple-element.28) | copy-start | bytes 3538948
  182.2 3.5 %copy-start.7 = (f32[8,1,192]{2,1,0:T(1,128)S(1)}, f32[8,1,192]{2,1,0:T(1,128)}, u32[]{:S(2)}) copy-start(f32[8,1,192]{2,1,0:T(1,128)} %get-tuple-element.29) | copy-start | bytes 18436
  184.8 3.2 %copy-start.6 = (f32[4,1,1024]{2,1,0:T(1,128)S(1)}, f32[4,1,1024]{2,1,0:T(1,128)}, u32[]{:S(2)}) copy-start(f32[4,1,1024]{2,1,0:T(1,128)} %get-tuple-element.25) | copy-start | bytes 49156

commit v3 on v2

--- a/solution.py
+++ b/solution.py
@@ -11,16 +11,32 @@
 MESH = pl.DeviceIdType.MESH
 
 
+def chunks_of(array):
+    return next(n for n in (3, 2, 1) if array.shape[0] % (16 * n) == 0 or n == 1)
+
+
 def exchange(collective_id, *parts):
     arrays = [part[0] for part in parts]
     axes = sorted({part[1] for part in parts})
     counts = {axis: lax.axis_size(axis) for axis in axes}
-    shapes, slots = [], []
+    shapes, slots, pairs = [], [], []
     for array, axis, kind in parts:
         count = counts[axis]
         lead = (count,) if kind in ("gather", "direct") else ()
-        shapes.append(jax.ShapeDtypeStruct(lead + array.shape, array.dtype))
-        slots.append({"scatter": count, "direct": count, "gather": 2 * count}.get(kind, 1))
+        shape = lead + array.shape
+        if kind == "reduce":
+            shape = (count // 2,) + array.shape[1:]
+            pairs.append(pltpu.VMEM(shape, array.dtype))
+            pairs.append(pltpu.VMEM(shape, array.dtype))
+        shapes.append(jax.ShapeDtypeStruct(shape, array.dtype))
+        slots.append(
+            {
+                "scatter": count,
+                "direct": count,
+                "reduce": count,
+                "gather": 2 * count * chunks_of(array),
+            }.get(kind, 1)
+        )
     number = len(parts)
 
     def remote(source, target, sends, receives, slot, axis, peer):
@@ -49,7 +65,64 @@
             for copy in copies:
                 copy.wait()
 
-        return (lambda: None), finish
+        return (lambda step: None), finish
+
+    def reduce(source, target, sends, receives, axis, came, summed):
+        here, count = lax.axis_index(axis), counts[axis]
+        line = count // 2
+        outer, inner = here // 2, lax.rem(here, 2)
+        order = [*range(1, line), 0]
+
+        def place(step):
+            return lax.rem(outer + step, line)
+
+        def to_partner(step):
+            there = place(step)
+            return remote(
+                source.at[2 * there + 1 - inner],
+                came.at[there],
+                sends,
+                receives,
+                step,
+                axis,
+                2 * outer + 1 - inner,
+            )
+
+        def to_owner(step):
+            there = place(step)
+            return remote(
+                summed.at[there],
+                target.at[outer],
+                sends,
+                receives,
+                line + step,
+                axis,
+                2 * there + inner,
+            )
+
+        for step in order:
+            to_partner(step).start()
+
+        def relay(turn):
+            if turn > line:
+                return
+            step = order[turn - 1]
+            there = place(step)
+            to_partner(step).wait_recv()
+            pair = source[2 * there + inner].astype(jnp.float32) + came[there].astype(jnp.float32)
+            if step:
+                summed[there] = pair.astype(summed.dtype)
+                to_owner(step).start()
+            else:
+                target[outer] = pair.astype(target.dtype)
+
+        def finish():
+            for step in order:
+                to_partner(step).wait_send()
+                if step:
+                    to_owner(step).wait()
+
+        return relay, finish
 
     def shift(source, target, sends, receives, axis, forward):
         here, count = lax.axis_index(axis), counts[axis]
@@ -64,30 +137,33 @@
             pl.when(has_peer)(copy.wait_send)
             pl.when(has_source)(copy.wait_recv)
 
-        return (lambda: None), finish
-
-    def gather(source, target, sends, receives, axis):
+        return (lambda step: None), finish
+
+    def gather(source, target, sends, receives, axis, chunk, height):
+        base = 2 * counts[axis] * chunk
+        piece = pl.ds(chunk * height, height)
+        source, whole = source.at[piece], target
         here, count = lax.axis_index(axis), counts[axis]
         line = count // 2
         outer = here // 2
         partner = here + 1 - 2 * lax.rem(here, 2)
         ahead = lax.rem(here + 2, count)
         behind = lax.rem(here + count - 2, count)
-        own = pltpu.make_async_copy(source, target.at[here], sends.at[0])
+        own = pltpu.make_async_copy(source, whole.at[here, piece], sends.at[base + line])
 
         def block(shift):
-            return target.at[lax.rem(here + 2 * shift + count, count)]
+            return whole.at[lax.rem(here + 2 * shift + count, count), piece]
 
         def hand_on(shift, direction, step):
             peer = ahead if direction > 0 else behind
             slot = step if direction > 0 else line + step
             taken = source if shift == 0 else block(shift)
-            return remote(taken, block(shift), sends, receives, slot, axis, peer)
+            return remote(taken, block(shift), sends, receives, base + slot, axis, peer)
 
         def hand_over(shift):
             slot = 2 * line + (shift if shift >= 0 else line - 1 - shift)
             taken = source if shift == 0 else block(shift)
-            return remote(taken, block(shift), sends, receives, slot, axis, partner)
+            return remote(taken, block(shift), sends, receives, base + slot, axis, partner)
 
         def there(shift):
             place = outer + shift
@@ -99,8 +175,8 @@
         hand_over(0).start()
         own.start()
 
-        def relay():
-            for step in range(1, line):
+        def relay(step):
+            if step < line:
                 for direction in (1, -1):
                     came = -direction * step
 
@@ -142,15 +218,21 @@
                 expected += 1
         pl.semaphore_wait(barrier, expected)
         pending = []
-        for (_, axis, kind), *held in zip(parts, *groups):
+        scratch = list(refs[4 * number :])
+        for (array, axis, kind), *held in zip(parts, *groups):
             if kind in ("scatter", "direct"):
                 pending.append(scatter(*held, axis, kind == "scatter"))
             elif kind == "gather":
-                pending.append(gather(*held, axis))
+                chunks = chunks_of(array)
+                for chunk in range(chunks):
+                    pending.append(gather(*held, axis, chunk, array.shape[0] // chunks))
+            elif kind == "reduce":
+                pending.append(reduce(*held, axis, scratch.pop(0), scratch.pop(0)))
             else:
                 pending.append(shift(*held, axis, kind == "next"))
-        for relay, _ in pending:
-            relay()
+        for step in range(1, max(counts.values()) // 2 + 1):
+            for relay, _ in pending:
+                relay(step)
         for _, finish in pending:
             finish()
 
@@ -159,7 +241,7 @@
         out_shape=shapes,
         in_specs=[pl.BlockSpec(memory_space=pltpu.VMEM)] * number,
         out_specs=[pl.BlockSpec(memory_space=pltpu.VMEM)] * number,
-        scratch_shapes=[pltpu.SemaphoreType.DMA((n,)) for n in slots] * 2,
+        scratch_shapes=[pltpu.SemaphoreType.DMA((n,)) for n in slots] * 2 + pairs,
         compiler_params=pltpu.CompilerParams(collective_id=collective_id, has_side_effects=True),
         name=f"exchange_{collective_id}",
     )(*arrays)
@@ -342,7 +424,7 @@
         4,
         (dots_part, "mp", "direct"),
         (gain_part, "mp", "scatter"),
-        (weight_part, "seg", "scatter"),
+        (weight_part, "seg", "reduce"),
         (shared_hidden, "mp", "scatter"),
     )
     factor = (tok_rows * segments) ** (-0.5)

time: 192 us -> 182 us (0.948)
  Pallas kernels: 142 us -> 133 us
    pallas_call x6, Pallas kernels: 115 us -> 106 us  [exchange(): pl.pallas_call(body, out_shape=shapes, in_specs=[pl.BlockSpec(memory_spac...]
where the time goes in v3:
time: 182 us; the launch traced here: 181 us
  Pallas kernels  133 us (73%)
  matrix products  19.2 us (11%)
  other arithmetic  15.3 us (8%)
  local copies, waits for them, and re-layouts  12.7 us (7%)
    pallas_call x6, Pallas kernels, exchange(): pl.pallas_call(body, out_shape=shapes, in_specs=[pl.BlockSpec(memory_spac...  106 us
    pallas_call x1, Pallas kernels, attention(): pl.pallas_call(body, grid=(tok_rows // rows,), in_specs=[by_row, whole, b...  27.1 us

profile of v3, /device:TPU:0, one launch (start us, length us, event | category | flops | bytes accessed | tf_op | source)
XLA Modules:
  0.0 181.1 jit_solution(14217541944317239312)
XLA Ops:
  0.7 1.3 fusion.10
  2.0 0.7 convert_add_fusion.1
  2.6 3.3 %fusion.5 = bf16[192,2048]{1,0:T(8,128)(2,1)S(1)} fusion(s32[1024]{0:T(1024)S(1)} %convert_add_fusion.1, bf16[1024,768]{1,0:T(8,128)(2,1)} %param.10, s32[]{:T(128)S(6)} %select_n.32), kind=kOutput, calls=%fused_computation.15 | convolution fusion | flops 807796736 | bytes 1314820 | tf_op jit(solution)/shard_map/dot_general | solution.py:352
  6.0 0.9 copy.41
  6.9 20.8 %exchange_0.1 = bf16[8,192,256]{2,1,0:T(8,128)(2,1)} custom-call(bf16[8,192,256]{2,1,0:T(8,128)(2,1)} %bitcast.50), custom_call_target="tpu_custom_call" | custom-call | tf_op jit(solution)/shard_map/exchange_0/pallas_call | solution.py:239
  27.7 1.2 copy.39
  29.0 2.5 %fusion.8.refs_0_ = bf16[192,1024]{1,0:T(8,128)(2,1)} fusion(bf16[192,2048]{1,0:T(8,128)(2,1)S(1)} %bitcast.55, s32[1024]{0:T(1024)S(1)} %copy-done.16), kind=kOutput, calls=%fused_computation.21 | convolution fusion | flops 807600128 | bytes 1183744 | tf_op jit(solution)/shard_map/dot_general | solution.py:359
  31.5 15.0 %exchange_1.1 = bf16[4,192,1024]{2,1,0:T(8,128)(2,1)} custom-call(bf16[192,1024]{1,0:T(8,128)(2,1)} %fusion.8.refs_0_), custom_call_target="tpu_custom_call" | custom-call | tf_op jit(solution)/shard_map/exchange_1/pallas_call | solution.py:239
  46.5 2.2 %multiply_reduce_fusion.1 = (f32[1024]{0:T(1024)S(1)}, f32[1024,768]{0,1:T(8,128)S(1)}) fusion(bf16[4,192,1024]{2,1,0:T(8,128)(2,1)} %exchange_1.1, bf16[4,768]{1,0:T(4,128)(2,1)S(1)} %copy-done.8, s32[1024]{0:T(1024)S(1)} %copy-done.9), kind=kOutput, calls=%fused_computation.14 | convolution fusion | flops 9440256 | bytes 4732928 | tf_op jit(solution)/shard_map/dot_general | solution.py:365
  48.8 0.9 fusion.6
  49.7 0.3 copy-done.11
  49.9 1.7 convolution_convert_fusion
  51.6 0.8 fusion.19
  52.4 14.8 %exchange_2.1 = (bf16[128,384]{1,0:T(8,128)(2,1)}, bf16[128,384]{1,0:T(8,128)(2,1)}) custom-call(bf16[128,384]{1,0:T(8,128)(2,1)} %get-tuple-element.35.refs_0_, bf16[128,384]{1,0:T(8,128)(2,1)} %get-tuple-element.34.refs_1_), custom_call_target="tpu_custom_call" | custom-call | tf_op jit(solution)/shard_map/exchange_2/pallas_call | solution.py:239
  67.2 0.9 broadcast_select_fusion
  68.1 0.3 slice.60
  68.5 1.0 pad_maximum_fusion.1.kv_ref
  69.5 0.8 slice.57.q_ref
  70.3 0.7 convolution_convert_fusion.2
  71.0 1.0 copy.34.g_ref
  72.0 1.0 copy.35.near_ref
  73.0 27.1 %window_attention.1 = (bf16[1024,192]{1,0:T(8,128)(2,1)}, bf16[1024,192]{1,0:T(8,128)(2,1)}, f32[1280,384]{1,0:T(8,128)}) custom-call(bf16[1024,192]{1,0:T(8,128)(2,1)} %slice.57.q_ref, bf16[1280,384]{1,0:T(8,128)(2,1)} %pad_maximum_fusion.1.kv_ref, bf16[1024,192]{1,0:T(8,128)(2,1)} %copy.34.g_ref, s32[1024,16]{1,0:T(8,128)} %copy.35.near_ref), custom_call_target="tpu_custom_call" | custom-call | tf_op jit(solution)/shard_map/window_attention/pallas_call | solution.py:301
  100.2 1.7 convert.13
  101.9 0.7 fusion.20
  102.6 8.5 %exchange_3.1 = (bf16[128,384]{1,0:T(8,128)(2,1)}, bf16[128,384]{1,0:T(8,128)(2,1)}) custom-call(bf16[128,384]{1,0:T(8,128)(2,1)} %get-tuple-element.37.refs_0_, bf16[128,384]{1,0:T(8,128)(2,1)} %get-tuple-element.36.refs_1_), custom_call_target="tpu_custom_call" | custom-call | tf_op jit(solution)/shard_map/exchange_3/pallas_call | solution.py:239
  111.1 1.1 add_convert_fusion.1
  112.3 0.1 slice.63
  112.4 3.6 %convolution_convert_fusion.1 = bf16[576,768]{1,0:T(8,128)(2,1)S(1)} fusion(bf16[128,384]{1,0:T(8,128)(2,1)S(1)} %get-tuple-element.33, bf16[768,384]{1,0:T(8,128)(2,1)S(1)} %slice.63, bf16[128,384]{1,0:T(8,128)(2,1)S(1)} %get-tuple-element.32, bf16[1024,192]{1,0:T(8,128)(2,1)S(1)} %copy-done.13, f32[768,1024]{1,0:T(8,128)} %copy-done.2, f32[768]{0:T(1024)S(1)} %copy-done.10), kind=kOutput, calls=%fused_computation.18 | convolution fusion | flops 912703488 | bytes 5213184 | tf_op jit(solution)/shard_map/dot_general | solution.py:406
  116.0 0.5 convolution_convert_fusion.3
  116.5 1.1 pad_maximum_fusion
  117.7 0.6 copy-done.3
  118.3 0.2 copy-done.12
  118.5 3.4 %fusion.7 = (f32[768]{0:T(1024)S(1)}, f32[1024]{0:T(1024)}, bf16[1024,768]{0,1:T(8,128)(2,1)}) fusion(f32[768,1024]{1,0:T(8,128)S(1)} %copy-done.3, f32[768]{0:T(1024)S(1)} %copy-done.10, bf16[768,576]{0,1:T(8,128)(2,1)S(1)} %bitcast.60, bf16[128,384]{1,0:T(8,128)(2,1)S(1)} %get-tuple-element.33, bf16[768,384]{1,0:T(8,128)(2,1)S(1)} %slice.63, ...), kind=kOutput, calls=%fused_computation.19 | convolution fusion | flops 914618624 | bytes 6793216 | tf_op jit(solution)/shard_map/dot_general | solution.py:416
  122.0 0.7 reshape.73.refs_1_
  122.6 26.2 %exchange_4.1 = (f32[4,1,1024]{2,1,0:T(1,128)}, f32[4,1,192]{2,1,0:T(1,128)}, bf16[4,96,768]{2,1,0:T(8,128)(2,1)}, bf16[4,192,1024]{2,1,0:T(8,128)(2,1)}) custom-call(f32[1,1024]{1,0:T(1,128)} %bitcast.57, f32[4,1,192]{2,1,0:T(1,128)} %reshape.73.refs_1_, bf16[8,96,768]{2,1,0:T(8,128)(2,1)} %bitcast.49, bf16[4,192,1024]{2,1,0:T(8,128)(2,1)} %bitcast.53), custom_call_target="tpu_custom_call" | custom-call | tf_op jit(solution)/shard_map/exchange_4/pallas_call | solution.py:239
  148.9 1.2 convert_reduce_fusion.1
  150.0 0.7 multiply_convert_fusion.1.refs_1_
  150.7 0.7 reduce_sum.87
  151.4 0.6 broadcast_multiply_fusion.1
  152.0 20.5 %exchange_5.1 = (f32[8,1,192]{2,1,0:T(1,128)}, bf16[8,96,768]{2,1,0:T(8,128)(2,1)}) custom-call(f32[1,192]{1,0:T(1,128)} %bitcast.58, bf16[96,768]{1,0:T(8,128)(2,1)} %multiply_convert_fusion.1.refs_1_), custom_call_target="tpu_custom_call" | custom-call | tf_op jit(solution)/shard_map/exchange_5/pallas_call | solution.py:239
  172.5 2.6 %slice.64 = f32[6,96,768]{2,1,0:T(8,128)} slice(bf16[8,96,768]{2,1,0:T(8,128)(2,1)} %get-tuple-element.28), slice={[0:6], [0:96], [0:768]} | slice | bytes 3538944 | tf_op jit(solution)/shard_map/slice | solution.py:435
  175.1 0.9 slice.65
  176.0 0.6 reduce_sum.89
  176.6 1.8 convert_reduce_fusion
  178.4 0.2 constant_dynamic-slice_fusion
  178.6 0.2 copy.37
  178.8 0.1 dynamic-slice.3
  178.9 2.2 %bitcast_add_fusion = f32[1024,192]{0,1:T(8,128)} fusion(f32[768,1024]{1,0:T(8,128)} %copy-done.2, s32[]{:T(128)S(6)} %select_n.32, f32[192,1024]{1,0:T(8,128)S(1)} %convert_reduce_fusion, bf16[1024,192]{0,1:T(8,128)(2,1)S(1)} %copy.37, f32[1024]{0:T(1024)S(1)} %broadcast_multiply_fusion, f32[192]{0:T(256)S(1)} %dynamic-slice.3, f32[1024]{0:T(1024)S(1)} %add_rsqrt_fusion), kind=kLoop, calls=%fused_computation.30 | loop fusion | flops 1179648 | bytes 2761476 | tf_op jit(solution)/shard_map/add | solution.py:442
  (34 shorter events, 0.1 us)
Async XLA Ops:
  0.6 69.7 %copy-start = (bf16[1024,768]{1,0:T(8,128)(2,1)S(1)}, bf16[1024,768]{1,0:T(8,128)(2,1)}, u32[]{:S(2)}) copy-start(bf16[1024,768]{1,0:T(8,128)(2,1)} %param.19) | copy-start | bytes 4718596
  6.0 23.0 %copy-start.16 = (s32[1024]{0:T(1024)S(1)}, s32[1024]{0:T(1024)}, u32[]{:S(2)}) copy-start(s32[1024]{0:T(1024)} %param.12) | copy-start | bytes 12292
  29.0 17.5 %copy-start.8 = (bf16[4,768]{1,0:T(4,128)(2,1)S(1)}, bf16[4,768]{1,0:T(4,128)(2,1)}, u32[]{:S(2)}) copy-start(bf16[4,768]{1,0:T(4,128)(2,1)} %param.15) | copy-start | bytes 18436
  29.0 17.5 %copy-start.9 = (s32[1024]{0:T(1024)S(1)}, s32[1024]{0:T(1024)}, u32[]{:S(2)}) copy-start(s32[1024]{0:T(1024)} %param.13) | copy-start | bytes 12292
  46.5 2.2 %copy-start.1 = (bf16[4,192,1024]{2,1,0:T(8,128)(2,1)S(1)}, bf16[4,192,1024]{2,1,0:T(8,128)(2,1)}, u32[]{:S(2)}) copy-start(bf16[4,192,1024]{2,1,0:T(8,128)(2,1)} %exchange_1.1) | copy-start | bytes 4718596
  48.7 0.9 copy-start.10
  48.7 1.2 copy-start.11
  49.6 1.9 %copy-start.2 = (f32[768,1024]{1,0:T(8,128)}, f32[768,1024]{1,0:T(8,128)S(1)}, u32[]{:S(2)}) copy-start(f32[768,1024]{1,0:T(8,128)S(1)} %fusion.6) | copy-start | bytes 9437188
  68.1 2.2 %copy-start.15 = (bf16[192,768]{1,0:T(8,128)(2,1)S(1)}, bf16[192,768]{1,0:T(8,128)(2,1)}, u32[]{:S(2)}) copy-start(bf16[192,768]{1,0:T(8,128)(2,1)} %param.18) | copy-start | bytes 884740
  69.5 2.5 %copy-start.5 = (s32[1024,16]{0,1:T(8,128)S(1)}, s32[1024,16]{0,1:T(8,128)}, u32[]{:S(2)}) copy-start(s32[1024,16]{0,1:T(8,128)} %param.14) | copy-start | bytes 196612
  100.2 12.2 %copy-start.13 = (bf16[1024,192]{1,0:T(8,128)(2,1)S(1)}, bf16[1024,192]{1,0:T(8,128)(2,1)}, u32[]{:S(2)}) copy-start(bf16[1024,192]{1,0:T(8,128)(2,1)} %get-tuple-element.19) | copy-start | bytes 1179652
  112.3 3.6 %copy-start.14 = (bf16[1024,192]{1,0:T(8,128)(2,1)S(1)}, bf16[1024,192]{1,0:T(8,128)(2,1)}, u32[]{:S(2)}) copy-start(bf16[1024,192]{1,0:T(8,128)(2,1)} %get-tuple-element.23) | copy-start | bytes 1179652
  116.0 2.3 %copy-start.3 = (f32[768,1024]{1,0:T(8,128)S(1)}, f32[768,1024]{1,0:T(8,128)}, u32[]{:S(2)}) copy-start(f32[768,1024]{1,0:T(8,128)} %copy-done.2) | copy-start | bytes 9437188
  116.0 2.5 %copy-start.12 = (bf16[768,3,192]{0,2,1:T(8,128)(2,1)S(1)}, bf16[768,3,192]{0,2,1:T(8,128)(2,1)}, u32[]{:S(2)}) copy-start(bf16[768,3,192]{0,2,1:T(8,128)(2,1)} %param.17) | copy-start | bytes 2654212
  172.5 2.6 %copy-start.4 = (bf16[8,96,768]{2,1,0:T(8,128)(2,1)S(1)}, bf16[8,96,768]{2,1,0:T(8,128)(2,1)}, u32[]{:S(2)}) copy-start(bf16[8,96,768]{2,1,0:T(8,128)(2,1)} %get-tuple-element.28) | copy-start | bytes 3538948
  172.5 3.5 %copy-start.7 = (f32[8,1,192]{2,1,0:T(1,128)S(1)}, f32[8,1,192]{2,1,0:T(1,128)}, u32[]{:S(2)}) copy-start(f32[8,1,192]{2,1,0:T(1,128)} %get-tuple-element.29) | copy-start | bytes 18436
  175.1 3.2 %copy-start.6 = (f32[4,1,1024]{2,1,0:T(1,128)S(1)}, f32[4,1,1024]{2,1,0:T(1,128)}, u32[]{:S(2)}) copy-start(f32[4,1,1024]{2,1,0:T(1,128)} %get-tuple-element.25) | copy-start | bytes 49156

commit v4 on v3

--- a/solution.py
+++ b/solution.py
@@ -425,7 +425,7 @@
         (dots_part, "mp", "direct"),
         (gain_part, "mp", "scatter"),
         (weight_part, "seg", "reduce"),
-        (shared_hidden, "mp", "scatter"),
+        (shared_hidden, "mp", "reduce"),
     )
     factor = (tok_rows * segments) ** (-0.5)
     weight_sum = (jnp.sum(weights_in.astype(f32), axis=0) * factor).astype(bf16)

time: 182 us -> 180 us (0.989)
  no operation moved by 1% of the time
where the time goes in v4:
time: 180 us; the launch traced here: 179 us
  Pallas kernels  133 us (74%)
  matrix products  19.2 us (11%)
  other arithmetic  13.6 us (8%)
  local copies, waits for them, and re-layouts  12.8 us (7%)
    pallas_call x6, Pallas kernels, exchange(): pl.pallas_call(body, out_shape=shapes, in_specs=[pl.BlockSpec(memory_spac...  105 us
    pallas_call x1, Pallas kernels, attention(): pl.pallas_call(body, grid=(tok_rows // rows,), in_specs=[by_row, whole, b...  27.2 us
    dot_general x1, matrix products, per_device(): lax.dot_general(grad_qkv, hidden, (((0,), (1,)), ((), ())), preferred_ele...  3.6 us

profile of v4, /device:TPU:0, one launch (start us, length us, event | category | flops | bytes accessed | tf_op | source)
XLA Modules:
  0.0 179.3 jit_solution(4033352606053375566)
XLA Ops:
  0.7 1.3 fusion.10
  2.0 0.7 convert_add_fusion.1
  2.6 3.3 %fusion.5 = bf16[192,2048]{1,0:T(8,128)(2,1)S(1)} fusion(s32[1024]{0:T(1024)S(1)} %convert_add_fusion.1, bf16[1024,768]{1,0:T(8,128)(2,1)} %param.10, s32[]{:T(128)S(6)} %select_n.32), kind=kOutput, calls=%fused_computation.14 | convolution fusion | flops 807796736 | bytes 1314820 | tf_op jit(solution)/shard_map/dot_general | solution.py:352
  6.0 0.9 copy.41
  6.9 20.8 %exchange_0.1 = bf16[8,192,256]{2,1,0:T(8,128)(2,1)} custom-call(bf16[8,192,256]{2,1,0:T(8,128)(2,1)} %bitcast.50), custom_call_target="tpu_custom_call" | custom-call | tf_op jit(solution)/shard_map/exchange_0/pallas_call | solution.py:239
  27.7 1.2 copy.39
  29.0 2.5 %fusion.8.refs_0_ = bf16[192,1024]{1,0:T(8,128)(2,1)} fusion(bf16[192,2048]{1,0:T(8,128)(2,1)S(1)} %bitcast.55, s32[1024]{0:T(1024)S(1)} %copy-done.17), kind=kOutput, calls=%fused_computation.21 | convolution fusion | flops 807600128 | bytes 1183744 | tf_op jit(solution)/shard_map/dot_general | solution.py:359
  31.5 15.0 %exchange_1.1 = bf16[4,192,1024]{2,1,0:T(8,128)(2,1)} custom-call(bf16[192,1024]{1,0:T(8,128)(2,1)} %fusion.8.refs_0_), custom_call_target="tpu_custom_call" | custom-call | tf_op jit(solution)/shard_map/exchange_1/pallas_call | solution.py:239
  46.6 2.2 %multiply_reduce_fusion.1 = (f32[1024]{0:T(1024)S(1)}, f32[1024,768]{0,1:T(8,128)S(1)}) fusion(bf16[4,192,1024]{2,1,0:T(8,128)(2,1)} %exchange_1.1, bf16[4,768]{1,0:T(4,128)(2,1)S(1)} %copy-done.9, s32[1024]{0:T(1024)S(1)} %copy-done.10), kind=kOutput, calls=%fused_computation.13 | convolution fusion | flops 9440256 | bytes 4732928 | tf_op jit(solution)/shard_map/dot_general | solution.py:365
  48.8 0.9 fusion.6
  49.7 0.3 copy-done.12
  50.0 1.7 convolution_convert_fusion
  51.6 0.8 fusion.19
  52.4 14.8 %exchange_2.1 = (bf16[128,384]{1,0:T(8,128)(2,1)}, bf16[128,384]{1,0:T(8,128)(2,1)}) custom-call(bf16[128,384]{1,0:T(8,128)(2,1)} %get-tuple-element.35.refs_0_, bf16[128,384]{1,0:T(8,128)(2,1)} %get-tuple-element.34.refs_1_), custom_call_target="tpu_custom_call" | custom-call | tf_op jit(solution)/shard_map/exchange_2/pallas_call | solution.py:239
  67.2 0.9 broadcast_select_fusion
  68.2 0.3 slice.60
  68.5 1.0 pad_maximum_fusion.1.kv_ref
  69.5 0.8 slice.57.q_ref
  70.4 0.7 convolution_convert_fusion.2
  71.0 1.0 copy.34.g_ref
  72.0 1.0 copy.35.near_ref
  73.1 27.2 %window_attention.1 = (bf16[1024,192]{1,0:T(8,128)(2,1)}, bf16[1024,192]{1,0:T(8,128)(2,1)}, f32[1280,384]{1,0:T(8,128)}) custom-call(bf16[1024,192]{1,0:T(8,128)(2,1)} %slice.57.q_ref, bf16[1280,384]{1,0:T(8,128)(2,1)} %pad_maximum_fusion.1.kv_ref, bf16[1024,192]{1,0:T(8,128)(2,1)} %copy.34.g_ref, s32[1024,16]{1,0:T(8,128)} %copy.35.near_ref), custom_call_target="tpu_custom_call" | custom-call | tf_op jit(solution)/shard_map/window_attention/pallas_call | solution.py:301
  100.2 1.7 convert.13
  101.9 0.7 fusion.20
  102.6 8.5 %exchange_3.1 = (bf16[128,384]{1,0:T(8,128)(2,1)}, bf16[128,384]{1,0:T(8,128)(2,1)}) custom-call(bf16[128,384]{1,0:T(8,128)(2,1)} %get-tuple-element.37.refs_0_, bf16[128,384]{1,0:T(8,128)(2,1)} %get-tuple-element.36.refs_1_), custom_call_target="tpu_custom_call" | custom-call | tf_op jit(solution)/shard_map/exchange_3/pallas_call | solution.py:239
  111.2 1.1 add_convert_fusion.1
  112.3 0.1 slice.63
  112.4 3.6 %convolution_convert_fusion.1 = bf16[576,768]{1,0:T(8,128)(2,1)S(1)} fusion(bf16[128,384]{1,0:T(8,128)(2,1)S(1)} %get-tuple-element.33, bf16[768,384]{1,0:T(8,128)(2,1)S(1)} %slice.63, bf16[128,384]{1,0:T(8,128)(2,1)S(1)} %get-tuple-element.32, bf16[1024,192]{1,0:T(8,128)(2,1)S(1)} %copy-done.14, f32[768,1024]{1,0:T(8,128)} %copy-done.2, f32[768]{0:T(1024)S(1)} %copy-done.11), kind=kOutput, calls=%fused_computation.18 | convolution fusion | flops 912703488 | bytes 5213184 | tf_op jit(solution)/shard_map/dot_general | solution.py:406
  116.0 0.5 convolution_convert_fusion.3
  116.5 1.1 pad_maximum_fusion
  117.6 0.7 copy-done.3
  118.3 0.2 copy-done.13
  118.5 3.4 %fusion.7 = (f32[768]{0:T(1024)S(1)}, f32[1024]{0:T(1024)}, bf16[1024,768]{0,1:T(8,128)(2,1)}) fusion(f32[768,1024]{1,0:T(8,128)S(1)} %copy-done.3, f32[768]{0:T(1024)S(1)} %copy-done.11, bf16[768,576]{0,1:T(8,128)(2,1)S(1)} %bitcast.60, bf16[128,384]{1,0:T(8,128)(2,1)S(1)} %get-tuple-element.33, bf16[768,384]{1,0:T(8,128)(2,1)S(1)} %slice.63, ...), kind=kOutput, calls=%fused_computation.19 | convolution fusion | flops 914618624 | bytes 6793216 | tf_op jit(solution)/shard_map/dot_general | solution.py:416
  122.0 0.7 reshape.73.refs_1_
  122.7 26.0 %exchange_4.1 = (f32[4,1,1024]{2,1,0:T(1,128)}, f32[4,1,192]{2,1,0:T(1,128)}, bf16[4,96,768]{2,1,0:T(8,128)(2,1)}, bf16[2,192,1024]{2,1,0:T(8,128)(2,1)}) custom-call(f32[1,1024]{1,0:T(1,128)} %bitcast.57, f32[4,1,192]{2,1,0:T(1,128)} %reshape.73.refs_1_, bf16[8,96,768]{2,1,0:T(8,128)(2,1)} %bitcast.49, bf16[4,192,1024]{2,1,0:T(8,128)(2,1)} %bitcast.53), custom_call_target="tpu_custom_call" | custom-call | tf_op jit(solution)/shard_map/exchange_4/pallas_call | solution.py:239
  148.6 1.2 convert_reduce_fusion.1
  149.8 0.7 multiply_convert_fusion.1.refs_1_
  150.5 0.7 reduce_sum.87
  151.2 0.6 broadcast_multiply_fusion.1
  151.7 20.4 %exchange_5.1 = (f32[8,1,192]{2,1,0:T(1,128)}, bf16[8,96,768]{2,1,0:T(8,128)(2,1)}) custom-call(f32[1,192]{1,0:T(1,128)} %bitcast.58, bf16[96,768]{1,0:T(8,128)(2,1)} %multiply_convert_fusion.1.refs_1_), custom_call_target="tpu_custom_call" | custom-call | tf_op jit(solution)/shard_map/exchange_5/pallas_call | solution.py:239
  172.2 2.7 %slice.64 = f32[6,96,768]{2,1,0:T(8,128)} slice(bf16[8,96,768]{2,1,0:T(8,128)(2,1)} %get-tuple-element.28), slice={[0:6], [0:96], [0:768]} | slice | bytes 3538944 | tf_op jit(solution)/shard_map/slice | solution.py:435
  174.9 0.9 slice.65
  175.7 0.6 reduce_sum.89
  176.3 0.1 convert_reduce_fusion
  176.5 0.2 constant_dynamic-slice_fusion
  176.8 0.2 copy.37
  177.0 0.1 dynamic-slice.3
  177.0 2.2 %bitcast_add_fusion = f32[1024,192]{0,1:T(8,128)} fusion(f32[768,1024]{1,0:T(8,128)} %copy-done.2, s32[]{:T(128)S(6)} %select_n.32, f32[192,1024]{1,0:T(8,128)S(1)} %convert_reduce_fusion, bf16[1024,192]{0,1:T(8,128)(2,1)S(1)} %copy.37, f32[1024]{0:T(1024)S(1)} %broadcast_multiply_fusion, f32[192]{0:T(256)S(1)} %dynamic-slice.3, f32[1024]{0:T(1024)S(1)} %add_rsqrt_fusion), kind=kLoop, calls=%fused_computation.30 | loop fusion | flops 1179648 | bytes 2761476 | tf_op jit(solution)/shard_map/add | solution.py:442
  (36 shorter events, 0.1 us)
Async XLA Ops:
  0.6 69.7 %copy-start = (bf16[1024,768]{1,0:T(8,128)(2,1)S(1)}, bf16[1024,768]{1,0:T(8,128)(2,1)}, u32[]{:S(2)}) copy-start(bf16[1024,768]{1,0:T(8,128)(2,1)} %param.19) | copy-start | bytes 4718596
  6.0 23.0 %copy-start.17 = (s32[1024]{0:T(1024)S(1)}, s32[1024]{0:T(1024)}, u32[]{:S(2)}) copy-start(s32[1024]{0:T(1024)} %param.12) | copy-start | bytes 12292
  29.0 17.6 %copy-start.9 = (bf16[4,768]{1,0:T(4,128)(2,1)S(1)}, bf16[4,768]{1,0:T(4,128)(2,1)}, u32[]{:S(2)}) copy-start(bf16[4,768]{1,0:T(4,128)(2,1)} %param.15) | copy-start | bytes 18436
  29.0 17.6 %copy-start.10 = (s32[1024]{0:T(1024)S(1)}, s32[1024]{0:T(1024)}, u32[]{:S(2)}) copy-start(s32[1024]{0:T(1024)} %param.13) | copy-start | bytes 12292
  46.5 2.2 %copy-start.1 = (bf16[4,192,1024]{2,1,0:T(8,128)(2,1)S(1)}, bf16[4,192,1024]{2,1,0:T(8,128)(2,1)}, u32[]{:S(2)}) copy-start(bf16[4,192,1024]{2,1,0:T(8,128)(2,1)} %exchange_1.1) | copy-start | bytes 4718596
  48.8 0.9 copy-start.11
  48.8 1.2 copy-start.12
  49.7 1.9 %copy-start.2 = (f32[768,1024]{1,0:T(8,128)}, f32[768,1024]{1,0:T(8,128)S(1)}, u32[]{:S(2)}) copy-start(f32[768,1024]{1,0:T(8,128)S(1)} %fusion.6) | copy-start | bytes 9437188
  68.2 2.2 %copy-start.16 = (bf16[192,768]{1,0:T(8,128)(2,1)S(1)}, bf16[192,768]{1,0:T(8,128)(2,1)}, u32[]{:S(2)}) copy-start(bf16[192,768]{1,0:T(8,128)(2,1)} %param.18) | copy-start | bytes 884740
  69.5 2.5 %copy-start.6 = (s32[1024,16]{0,1:T(8,128)S(1)}, s32[1024,16]{0,1:T(8,128)}, u32[]{:S(2)}) copy-start(s32[1024,16]{0,1:T(8,128)} %param.14) | copy-start | bytes 196612
  100.2 12.2 %copy-start.14 = (bf16[1024,192]{1,0:T(8,128)(2,1)S(1)}, bf16[1024,192]{1,0:T(8,128)(2,1)}, u32[]{:S(2)}) copy-start(bf16[1024,192]{1,0:T(8,128)(2,1)} %get-tuple-element.19) | copy-start | bytes 1179652
  112.4 3.6 %copy-start.15 = (bf16[1024,192]{1,0:T(8,128)(2,1)S(1)}, bf16[1024,192]{1,0:T(8,128)(2,1)}, u32[]{:S(2)}) copy-start(bf16[1024,192]{1,0:T(8,128)(2,1)} %get-tuple-element.23) | copy-start | bytes 1179652
  116.0 2.3 %copy-start.3 = (f32[768,1024]{1,0:T(8,128)S(1)}, f32[768,1024]{1,0:T(8,128)}, u32[]{:S(2)}) copy-start(f32[768,1024]{1,0:T(8,128)} %copy-done.2) | copy-start | bytes 9437188
  116.0 2.5 %copy-start.13 = (bf16[768,3,192]{0,2,1:T(8,128)(2,1)S(1)}, bf16[768,3,192]{0,2,1:T(8,128)(2,1)}, u32[]{:S(2)}) copy-start(bf16[768,3,192]{0,2,1:T(8,128)(2,1)} %param.17) | copy-start | bytes 2654212
  172.2 2.7 %copy-start.4 = (bf16[8,96,768]{2,1,0:T(8,128)(2,1)S(1)}, bf16[8,96,768]{2,1,0:T(8,128)(2,1)}, u32[]{:S(2)}) copy-start(bf16[8,96,768]{2,1,0:T(8,128)(2,1)} %get-tuple-element.28) | copy-start | bytes 3538948
  172.2 3.5 %copy-start.8 = (f32[8,1,192]{2,1,0:T(1,128)S(1)}, f32[8,1,192]{2,1,0:T(1,128)}, u32[]{:S(2)}) copy-start(f32[8,1,192]{2,1,0:T(1,128)} %get-tuple-element.29) | copy-start | bytes 18436
  172.2 4.1 %copy-start.5 = (bf16[2,192,1024]{2,1,0:T(8,128)(2,1)S(1)}, bf16[2,192,1024]{2,1,0:T(8,128)(2,1)}, u32[]{:S(2)}) copy-start(bf16[2,192,1024]{2,1,0:T(8,128)(2,1)} %get-tuple-element.24) | copy-start | bytes 2359300
  174.9 1.6 copy-start.7
